TPU v7x, 256 devices: a whole 4x4x8 slice. The times are simulated.
256 devices in a mesh: tm: 32 (over x, z), chan: 8 (over y, core).
Axes of the slice: x: 4, y: 4, z: 8, core: 2. Of those that a mesh axis runs over, the one named last changes fastest.
Arguments:
- visibilities: bfloat16 [32, 8, 512, 1024], P('tm', None, None, 'chan'), may hold values from -6 to 6
- station_gains: float32 [8, 192, 1024], P(None, 'chan'), may hold values from -1.5 to 1.5, as said below
- station_pairs: int32 [512, 2], replicated, may hold values from 0 to 191, as said below
- average_bands: int32 [512, 2], replicated, may hold values from 0 to 3, as said below
- tile_map: int32 [512, 32], replicated, may hold values from 0 to 255
- baseline_order: int32 [512], replicated, may hold values from 0 to 511, as said below
Outputs:
- averaged: bfloat16 [32, 8, 512, 1024], P(None, None, 'tm', 'chan')
- gridded: float32 [256, 8, 1024], P('tm', None, 'chan')
Inputs may be any that keep to these rules, and one draw needn't show every extreme that they name: `station_pairs`: row b holds the two stations of baseline b, the first smaller than the second. `average_bands`: column 0 is at most 3, column 1 at most 2. In each aligned block of 16 positions k of baseline_order, the bands of the baselines baseline_order[k] are, in some order, the pairs (3 - j % (3 + 1), 2 - j % (2 + 1)) for j = 0 to 15. `baseline_order`: each baseline once. `station_gains`: diagonal Jones entries have magnitudes of order one.
All inputs are finite; a program needn't handle non-finite values.
Results may differ from a plain program's by a relative error of at most 0.019.
Values may be sent and summed in bfloat16 or wider, within the bound.
No kernel may reach another device: no remote copies, remote signals or barrier semaphores. Data moves between devices by JAX's collectives and lax.ppermute only.
A program may use at most 128 MiB of HBM per device.

v0:
```python
import jax
import jax.numpy as jnp
from jax import lax
from jax.sharding import PartitionSpec as P

TILE_DEV = 8
TLOG = 3
CLOG = 2


def product(left, right):
    return (left[0] * right[0] - left[1] * right[1], left[0] * right[1] + left[1] * right[0])


def product_conj(left, right):
    return (left[0] * right[0] + left[1] * right[1], left[1] * right[0] - left[0] * right[1])


def add_pair(left, right):
    return (left[0] + right[0], left[1] + right[1])


def as_matrix(components):
    return [
        [(components[0], components[1]), (components[2], components[3])],
        [(components[4], components[5]), (components[6], components[7])],
    ]


def jones_apply(first, middle, second):
    left_gain = as_matrix(first)
    coherency = as_matrix(middle)
    right_gain = as_matrix(second)
    partial_rows = [
        [
            add_pair(
                product(left_gain[i][0], coherency[0][k]), product(left_gain[i][1], coherency[1][k])
            )
            for k in range(2)
        ]
        for i in range(2)
    ]
    result = []
    for i in range(2):
        for c in range(2):
            element = add_pair(
                product_conj(partial_rows[i][0], right_gain[c][0]),
                product_conj(partial_rows[i][1], right_gain[c][1]),
            )
            result.extend(element)
    return result


def calibrate(samples, gain_table, first_station, second_station):
    left_gain = jnp.take(gain_table, first_station, axis=1)
    right_gain = jnp.take(gain_table, second_station, axis=1)
    values = [samples[:, i].astype(jnp.float32) for i in range(8)]
    result = jones_apply(
        [left_gain[i][None] for i in range(8)], values, [right_gain[i][None] for i in range(8)]
    )
    return jnp.stack(result, axis=1).astype(jnp.bfloat16)


def halve_time(current, size):
    extent = current.shape[0]
    shaped = current.reshape((extent // size, 2, size // 2) + current.shape[1:])
    merged = 0.5 * (shaped[:, 0:1] + shaped[:, 1:2])
    return jnp.broadcast_to(merged, shaped.shape).reshape(current.shape)


def halve_chan(current, size):
    extent = current.shape[-1]
    shaped = current.reshape(current.shape[:-1] + (extent // size, 2, size // 2))
    merged = 0.5 * (shaped[..., 0:1, :] + shaped[..., 1:2, :])
    return jnp.broadcast_to(merged, shaped.shape).reshape(current.shape)


def band_average(samples, time_levels, chan_levels):
    values = samples.astype(jnp.float32)
    time_select = time_levels[None, None, :, None]
    chan_select = chan_levels[None, None, :, None]
    result = values
    current = values
    for k in range(1, TLOG + 1):
        current = halve_time(current, 2**k)
        result = jnp.where(time_select >= k, current, result)
    final = result
    current = result
    for k in range(1, CLOG + 1):
        current = halve_chan(current, 2**k)
        final = jnp.where(chan_select >= k, current, final)
    return final.astype(jnp.bfloat16)


def shards(visibilities, station_gains, station_pairs, average_bands, tile_map, baseline_order):
    chan_width = visibilities.shape[3]
    block_size = visibilities.shape[2] // lax.axis_size("tm")
    all_gains = lax.all_gather(station_gains, "chan", axis=1, tiled=True)
    gain_table = lax.dynamic_slice_in_dim(
        all_gains, lax.axis_index("chan") * chan_width, chan_width, 2
    )
    reordered = jnp.take(visibilities, baseline_order, axis=2)
    rows_here = lax.dynamic_slice_in_dim(
        baseline_order, lax.axis_index("tm") * block_size, block_size
    )
    bands_here = average_bands[rows_here]
    ordered_pairs = station_pairs[baseline_order]
    payload = calibrate(reordered, gain_table, ordered_pairs[:, 0], ordered_pairs[:, 1])
    turned = lax.all_to_all(payload, "tm", split_axis=2, concat_axis=0, tiled=True)
    averaged = band_average(turned, bands_here[:, 0], bands_here[:, 1])
    tile_here = tile_map[rows_here].T
    time_index = jnp.arange(averaged.shape[0], dtype=jnp.int32)[:, None]
    period = jnp.left_shift(jnp.ones_like(bands_here[:, 0]), bands_here[:, 0])[None, :]
    tile_ids = jnp.where(time_index % period == 0, tile_here, -1)
    targets = jnp.arange(TILE_DEV * lax.axis_size("tm"), dtype=jnp.int32)
    one_hot = (tile_ids[None] == targets[:, None, None]).astype(jnp.bfloat16)
    gridded = lax.psum_scatter(
        jnp.einsum("rtb,tkbc->rkc", one_hot, averaged, preferred_element_type=jnp.float32).astype(
            jnp.bfloat16
        ),
        "tm",
        scatter_dimension=0,
        tiled=True,
    ).astype(jnp.float32)
    return (averaged, gridded)


def solution(mesh):
    return jax.shard_map(
        shards,
        mesh=mesh,
        in_specs=(P("tm", None, None, "chan"), P(None, "chan", None), P(), P(), P(), P()),
        out_specs=(P(None, None, "tm", "chan"), P("tm", None, "chan")),
        check_vma=False,
    )
```

profile of v0, /device:TPU:32, one launch (start us, length us, event | category | flops | bytes accessed | tf_op | source)
XLA Modules:
  0.0 473.9 jit_solution(13990417689148985308)
XLA Ops:
  7.2 2.5 copy.586
  9.8 0.1 copy.585
  10.0 0.7 copy.639
  10.7 1.0 gather_fusion.1
  11.8 1.8 gather_fusion.2
  13.6 0.3 slice_reduce_fusion
  13.9 0.2 bitcast_select_fusion.1
  14.1 42.4 %all-gather.2.cloned.1.call-done = f32[8,192,1024]{2,0,1:T(8,128)} async-done(((f32[8,24,1024]{2,0,1:T(8,128)}), f32[8,192,1024]{2,0,1:T(8,128)}) %all-gather.2.cloned.1.call-update) | async-done | bytes 6291472 | tf_op jit(solution)/shard_map/all_gather | solution.py:98
  56.6 1.2 constant_dynamic-slice_fusion
  57.8 2.7 gather_fusion.5
  60.5 2.7 gather_fusion.4
  63.2 2.2 fusion.11
  65.4 0.5 fusion.12
  65.9 0.4 bitcast_dynamic-update-slice_fusion.7
  66.7 0.4 bitcast_dynamic-update-slice_fusion.3
  67.5 1.6 copy.591
  69.1 10.1 %all-to-all-start = ((bf16[1,8,512,128]{3,1,0,2:T(8,128)(2,1)}), bf16[1,8,512,128]{3,1,0,2:T(8,128)(2,1)S(1)}, u32[]{:S(2)}, u32[]{:S(2)}) async-start(bf16[1,8,512,128]{3,1,0,2:T(8,128)(2,1)} %copy.591), calls=%async_computation | async-start | bytes 2097152 | tf_op jit(solution)/shard_map/all_to_all | solution.py:109
  79.2 0.1 copy.584
  79.6 0.6 gather_fusion
  80.2 0.6 gather_fusion.3
  80.9 0.8 compare_reduce_fusion.4
  81.7 0.2 bitcast_select_fusion.2
  81.9 26.0 %all-to-all-done = bf16[1,8,512,128]{3,1,0,2:T(8,128)(2,1)S(1)} async-done(((bf16[1,8,512,128]{3,1,0,2:T(8,128)(2,1)}), bf16[1,8,512,128]{3,1,0,2:T(8,128)(2,1)S(1)}, u32[]{:S(2)}, u32[]{:S(2)}) %all-to-all-start) | async-done | bytes 1048608 | tf_op jit(solution)/shard_map/all_to_all | solution.py:109
  107.9 0.1 copy.592
  108.0 1.6 convert_bitcast_fusion
  109.6 0.2 convert.65
  109.8 1.1 fusion.59
  111.2 2.8 copy.621
  113.9 2.6 copy.620
  116.6 5.8 %add_multiply_fusion = f32[8,1,8,16,128]{3,2,4,0,1:T(8,128)} fusion(f32[8,1,8,16,128]{3,2,4,0,1:T(8,128)} %copy.620, f32[8,1,8,16,128]{3,2,4,0,1:T(8,128)} %copy.621), kind=kLoop, calls=%fused_computation.7 | loop fusion | flops 262144 | bytes 1572864 | tf_op jit(solution)/shard_map/mul | solution.py:67
  122.4 2.7 copy.625
  125.1 2.4 fusion.5
  127.5 0.6 copy.624
  128.2 6.6 %copy.598 = f32[32,1,8,16,128]{0,3,4,2,1:T(8,128)} copy(f32[32,1,8,16,128]{4,3,0,2,1:T(8,128)} %convert_bitcast_fusion) | data formatting | bytes 4194304 | tf_op jit(solution)/shard_map/convert_element_type | solution.py:79
  134.8 8.7 %copy.600 = f32[32,8,16,64,2,1]{3,2,5,4,1,0:T(8,128)} copy(f32[32,8,16,64,2,1]{0,2,4,3,1,5:T(8,128)} %bitcast.225) | data formatting | bytes 4194304 | tf_op jit(solution)/shard_map/convert_element_type | solution.py:79
  143.5 6.0 %copy.597 = f32[16,8,16,128]{2,1,3,0:T(8,128)} copy(f32[16,8,16,128]{3,2,0,1:T(8,128)} %fusion.59) | data formatting | bytes 2097152 | tf_op jit(solution)/shard_map/broadcast_in_dim | solution.py:68
  149.5 11.0 %broadcast_in_dim.122 = f32[16,2,8,16,128]{3,2,4,1,0:T(8,128)} broadcast(f32[16,8,16,128]{2,1,3,0:T(8,128)} %copy.597), dimensions={0,2,3,4} | broadcast | bytes 3145728 | tf_op jit(solution)/shard_map/broadcast_in_dim | solution.py:68
  160.5 11.9 %copy.599 = f32[32,8,16,64,2,1]{3,2,5,4,1,0:T(8,128)} copy(f32[32,8,16,64,2,1]{2,1,4,3,0,5:T(8,128)} %bitcast.219) | data formatting | bytes 4194304 | tf_op jit(solution)/shard_map/broadcast_in_dim | solution.py:68
  172.4 7.6 %broadcast_in_dim.117 = f32[4,2,4,8,16,128]{4,3,5,2,1,0:T(8,128)} broadcast(f32[4,8,16,128]{2,1,3,0:T(8,128)S(1)} %fusion.5), dimensions={0,3,4,5} | broadcast | bytes 2359296 | tf_op jit(solution)/shard_map/broadcast_in_dim | solution.py:68
  180.0 12.0 %copy.602 = f32[32,8,16,64,2,1]{3,2,5,4,1,0:T(8,128)} copy(f32[32,8,16,64,2,1]{2,1,4,3,0,5:T(8,128)} %bitcast.220) | data formatting | bytes 4194304 | tf_op jit(solution)/shard_map/reshape | solution.py:68
  192.0 10.2 %broadcast_in_dim.119 = f32[8,2,2,8,16,128]{4,3,5,2,1,0:T(8,128)} broadcast(f32[8,8,16,128]{2,1,3,0:T(8,128)} %bitcast.224), dimensions={0,3,4,5} | broadcast | bytes 2621440 | tf_op jit(solution)/shard_map/broadcast_in_dim | solution.py:68
  202.2 11.9 %copy.601 = f32[32,8,16,64,2,1]{3,2,5,4,1,0:T(8,128)} copy(f32[32,8,16,64,2,1]{2,1,4,3,0,5:T(8,128)} %bitcast.221) | data formatting | bytes 4194304 | tf_op jit(solution)/shard_map/reshape | solution.py:68
  214.1 8.0 %select_select_fusion = f32[32,8,16,64,2,1]{3,2,5,4,1,0:T(8,128)S(1)} fusion(f32[32,8,16,64,2,1]{3,2,5,4,1,0:T(8,128)} %copy.602, f32[32,8,16,64,2,1]{3,2,5,4,1,0:T(8,128)} %copy.601, f32[32,8,16,64,2,1]{3,2,5,4,1,0:T(8,128)} %copy.599, f32[32,8,16,64,2,1]{3,2,5,4,1,0:T(8,128)} %copy.600, pred[16]{0:T(512)(128)(4,1)S(1)} %get-tuple-element.31, ...), kind=kLoop, calls=%fused_computation.6 | loop fusion | flops 1572864 | bytes 10485808 | tf_op jit(solution)/shard_map/jit(_where)/select_n | solution.py:86
  222.2 1.7 fusion.58
  223.9 0.4 fusion.2
  224.2 4.5 copy.606
  228.7 4.1 broadcast_in_dim.128
  232.8 6.1 %copy.610 = bf16[32,8,16,128]{3,2,0,1:T(8,128)(2,1)} copy(bf16[32,8,16,128]{0,2,3,1:T(8,128)(2,1)} %bitcast.228) | data formatting | bytes 2097152 | tf_op jit(solution)/shard_map/broadcast_in_dim | solution.py:75
  239.0 3.6 copy.603
  242.5 2.5 fusion.1
  245.1 2.5 broadcast_in_dim.125
  247.6 6.2 %copy.611 = bf16[32,8,16,128]{3,2,0,1:T(8,128)(2,1)} copy(bf16[32,8,16,128]{0,2,3,1:T(8,128)(2,1)} %bitcast.230) | data formatting | bytes 2097152 | tf_op jit(solution)/shard_map/reshape | solution.py:75
  253.8 0.1 broadcast_in_dim.122.clone
  254.0 0.1 broadcast_in_dim.119.clone
  254.1 0.1 broadcast_in_dim.117.clone
  254.3 0.8 copy-done.2
  255.0 0.3 copy-done.3
  255.3 1.0 fusion.10
  256.3 0.6 fusion.14
  256.9 0.9 copy.640
  257.9 1.3 copy.614
  259.1 206.6 %reduce-scatter.4.cloned.1.call-done = bf16[8,1024]{1,0:T(8,128)(2,1)} async-done(((bf16[256,1024]{1,0:T(8,128)(2,1)}), bf16[8,1024]{1,0:T(8,128)(2,1)}) %reduce-scatter.4.cloned.1.call-update) | async-done | bytes 16400
  465.7 0.7 bitcast_convert_fusion
  466.5 0.6 copy.615
  (49 shorter events, 1.5 us)
Async XLA Ops:
  7.2 2.7 copy-start.9
  7.2 2.8 copy-start.4
  7.2 3.5 copy-start.6
  7.2 49.4 %all-gather.2.cloned.1.call-start = ((), (), s32[]{:S(2)}) async-start(), calls=%async_computation.2 | async-start | bytes 7077888 | tf_op jit(solution)/shard_map/all_gather | solution.py:98
  63.2 2.2 copy-start.1
  67.4 11.8 %copy-start.10 = (s32[512,2]{0,1:T(2,128)S(1)}, s32[512,2]{0,1:T(2,128)}, u32[]{:S(2)}) copy-start(s32[512,2]{0,1:T(2,128)} %param.11) | copy-start | bytes 12292
  67.4 11.9 %copy-start.5 = (s32[512,32]{0,1:T(8,128)S(1)}, s32[512,32]{0,1:T(8,128)}, u32[]{:S(2)}) copy-start(s32[512,32]{0,1:T(8,128)} %param.12) | copy-start | bytes 196612
  69.1 38.8 %all-to-all-start = ((bf16[1,8,512,128]{3,1,0,2:T(8,128)(2,1)}), bf16[1,8,512,128]{3,1,0,2:T(8,128)(2,1)S(1)}, u32[]{:S(2)}, u32[]{:S(2)}) async-start(bf16[1,8,512,128]{3,1,0,2:T(8,128)(2,1)} %copy.591), calls=%async_computation | async-start | bytes 2097152 | tf_op jit(solution)/shard_map/all_to_all | solution.py:109
  79.2 386.6 %reduce-scatter.4.cloned.1.call-start = ((), (), s32[]{:S(2)}) async-start(), calls=%async_computation.3 | async-start | bytes 540672
  202.2 11.9 %copy-start.7 = (pred[16]{0:T(512)(128)(4,1)S(1)}, pred[16]{0:T(512)(128)(4,1)}, u32[]{:S(2)}) copy-start(pred[16]{0:T(512)(128)(4,1)} %get-tuple-element.33) | copy-start | bytes 52
  247.6 6.2 %copy-start = (f32[16,8,16,128]{3,2,0,1:T(8,128)S(1)}, f32[16,8,16,128]{3,2,0,1:T(8,128)}, u32[]{:S(2)}) copy-start(f32[16,8,16,128]{3,2,0,1:T(8,128)} %fusion.59) | copy-start | bytes 3145732
  253.8 1.2 copy-start.2
  253.8 1.5 copy-start.3
  253.8 1.5 copy-start.8
  253.8 1.5 copy-start.11
  253.8 1.5 copy-start.12
Sparse Core Ops, SparseCore 0:
  10.4 46.0 all-gather.1
  258.0 207.7 reduce-scatter.3
where the time goes:
time: 476 us; the launch traced here: 474 us
  waiting for transfers between devices  275 us (58%)
  local copies, waits for them, and re-layouts  142 us (30%)
  other arithmetic  31.2 us (7%)
  between operations  14.4 us (3%)
  starting transfers between devices  10.1 us (2%)
    unnamed x3, waiting for transfers between devices  207 us
    broadcast_in_dim x8, local copies, waits for them, and re-layouts, halve_time(): return jnp.broadcast_to(merged, shaped.shape).reshape(current.shape)  47.1 us
    all_gather x1, waiting for transfers between devices, shards(): all_gains = lax.all_gather(station_gains, 'chan', axis=1, tiled=True)  42.4 us
    all_to_all x1, waiting for transfers between devices, shards(): lax.all_to_all(payload, 'tm', split_axis=2, concat_axis=0, tiled=True)  26 us
    reshape x2, local copies, waits for them, and re-layouts, halve_time(): return jnp.broadcast_to(merged, shaped.shape).reshape(current.shape)  23.9 us
    broadcast_in_dim x4, local copies, waits for them, and re-layouts, halve_chan(): return jnp.broadcast_to(merged, shaped.shape).reshape(current.shape)  17.2 us
    unnamed x38, local copies, waits for them, and re-layouts  16.4 us
    convert_element_type x2, local copies, waits for them, and re-layouts, band_average(): values = samples.astype(jnp.float32)  15.3 us
  transfers between devices with their start and end apart: 3, of which 3 were waited for; matrix products, arithmetic and copies ran while one was open for 2% of the time, Pallas kernels for 0%

commit v1 on v0

v1 whole, which is shorter than its diff:
```python
import functools
import jax
import jax.numpy as jnp
from jax import lax
from jax.experimental import pallas as pl
from jax.experimental.pallas import tpu as pltpu
from jax.sharding import PartitionSpec as P

UNITS = (5, 5, 6)
BASE = (0, 5, 10)
ROW0 = (0, 40, 60)
ROWS = 72
F32 = jnp.float32
BF16 = jnp.bfloat16
VMEM_LIMIT = 24 << 20


def iota(shape, axis):
    return lax.broadcasted_iota(jnp.int32, shape, axis)


def one_hot(mask):
    return jnp.where(mask, 1.0, 0.0).astype(BF16)


def dot(a, b):
    return lax.dot_general(a, b, (((1,), (0,)), ((), ())), preferred_element_type=F32)


def dot_t(a, b):
    return lax.dot_general(a, b, (((1,), (1,)), ((), ())), preferred_element_type=F32)


def rows_of(values, width):
    row = iota((8, width), 0)
    result = jnp.zeros((8, width), F32)
    for i, value in enumerate(values):
        result = jnp.where(row == i, value, result)
    return result


def gains_kernel(gain_ref, out_ref):
    for d in range(8):
        out_ref[d] = gain_ref[:, :, d * 128 : (d + 1) * 128].astype(BF16)


def cut_gains(gains):
    comps, stations, _ = gains.shape
    return pl.pallas_call(
        gains_kernel,
        out_shape=jax.ShapeDtypeStruct((8, comps, stations, 128), BF16),
        compiler_params=pltpu.CompilerParams(vmem_limit_bytes=VMEM_LIMIT),
        name="cut_gains",
    )(gains)


def prepare_kernel(
    me_ref, pairs_ref, bands_ref, tiles_ref, order_ref, vis_ref,
    vis_out, left_out, right_out, weight_out, pick_out, lane_out, time_out,
):
    me = me_ref[0]
    nb = order_ref.shape[1]
    time_level = bands_ref[0:1, :]
    chan_level = bands_ref[1:2, :]
    tile = tiles_ref[pl.ds(me, 1), :]
    for level in range(1, 4):
        start = (me >> level) << level
        tile = jnp.where(time_level == level, tiles_ref[pl.ds(start, 1), :], tile)
    info = rows_of(
        [time_level.astype(F32), chan_level.astype(F32), tile.astype(F32)], nb
    ).astype(BF16)

    order_hot = one_hot(iota((nb, nb), 0) == order_ref[...])
    at_position = dot(info, order_hot)
    chan_here = at_position[1:2, :]
    same = rows_of([jnp.where(chan_here == float(level), 1.0, 0.0) for level in range(3)], nb)
    before = one_hot(
        (iota((nb, nb), 0) < iota((nb, nb), 1)) & ((iota((nb, nb), 0) >> 4) == (iota((nb, nb), 1) >> 4))
    )
    count = dot(same.astype(BF16), before)
    unit = jnp.where(
        chan_here == 0.0,
        count[0:1, :],
        jnp.where(chan_here == 1.0, BASE[1] + count[1:2, :], BASE[2] + count[2:3, :]),
    )
    block = iota((1, nb), 1) >> 4
    slot = unit.astype(jnp.int32) * 32 + block
    slot_hot = dot_t(one_hot(iota((nb, nb), 0) == slot), order_hot).astype(BF16)

    for c in range(0, 8, 2):
        both = jnp.concatenate([vis_ref[c], vis_ref[c + 1]], axis=1)
        moved = dot(slot_hot, both).astype(BF16)
        vis_out[c] = moved[:, :128]
        vis_out[c + 1] = moved[:, 128:]

    left_out[...] = dot_t(slot_hot, one_hot(iota((256, nb), 0) == pairs_ref[0:1, :])).astype(BF16)
    right_out[...] = dot_t(slot_hot, one_hot(iota((256, nb), 0) == pairs_ref[1:2, :])).astype(BF16)

    at_slot = dot_t(info, slot_hot)
    time_slot = at_slot[0:1, :]
    weight = jnp.where(
        time_slot == 0.0, 1.0, jnp.where(time_slot == 1.0, 0.5, jnp.where(time_slot == 2.0, 0.25, 0.125))
    )
    tile_slot = at_slot[2:3, :].astype(jnp.int32)
    weight_out[...] = jnp.where(iota((256, nb), 0) == tile_slot, weight, 0.0).astype(BF16)

    lane = iota((1, 128), 1)
    own = rows_of([at_position[0:1, :], chan_here, unit], nb).astype(BF16)
    own = dot(own, one_hot(iota((nb, 128), 0) == me * 16 + (iota((nb, 128), 1) & 15)))
    own_time = own[0:1, :]
    own_chan = own[1:2, :].astype(jnp.int32)
    own_unit = own[2:3, :].astype(jnp.int32)
    comp = lane >> 4
    packed_row = jnp.where(
        own_chan == 0,
        own_unit * 8 + comp,
        jnp.where(
            own_chan == 1,
            ROW0[1] + (own_unit - BASE[1]) * 4 + (comp >> 1),
            ROW0[2] + (own_unit - BASE[2]) * 2 + (comp >> 2),
        ),
    )
    part = jnp.where(own_chan == 0, 0, jnp.where(own_chan == 1, 1 + (comp & 1), 3 + (comp & 3)))
    sub = iota((128, 128), 0)
    lan = iota((128, 128), 1)
    eye = one_hot(sub == lan)
    row_hot = one_hot(sub == packed_row)
    pick_out[...] = dot_t(eye, row_hot).astype(BF16)
    part_hot = dot_t(eye, one_hot(sub == part)).astype(BF16)
    table = jnp.where(
        sub == 0,
        lan,
        jnp.where(sub <= 2, (sub - 1) * 64 + (lan >> 1), jnp.where(sub <= 6, (sub - 3) * 32 + (lan >> 2), 0)),
    )
    lane_out[...] = dot(part_hot, table.astype(F32).astype(BF16)).astype(jnp.int32)
    share = jnp.where(sub < ROW0[1], 1.0, jnp.where(sub < ROW0[2], 0.5, 0.25))
    spread = jnp.broadcast_to(own_time, (128, 128)).astype(BF16)
    time_out[...] = dot_t(row_hot, spread) * share


def prepare(me, pairs, bands, tiles, order, vis):
    nb = order.shape[1]
    vmem = pl.BlockSpec(memory_space=pltpu.VMEM)
    return pl.pallas_call(
        prepare_kernel,
        in_specs=[pl.BlockSpec(memory_space=pltpu.SMEM)] + [vmem] * 5,
        out_specs=[vmem] * 7,
        out_shape=[
            jax.ShapeDtypeStruct((8, nb, 128), BF16),
            jax.ShapeDtypeStruct((nb, 256), BF16),
            jax.ShapeDtypeStruct((nb, 256), BF16),
            jax.ShapeDtypeStruct((256, nb), BF16),
            jax.ShapeDtypeStruct((128, 128), BF16),
            jax.ShapeDtypeStruct((128, 128), jnp.int32),
            jax.ShapeDtypeStruct((128, 128), F32),
        ],
        compiler_params=pltpu.CompilerParams(vmem_limit_bytes=VMEM_LIMIT),
        cost_estimate=pl.CostEstimate(flops=2_000_000_000, bytes_accessed=4_000_000, transcendentals=0),
        name="prepare",
    )(me, pairs, bands, tiles, order, vis)


def product(left, right):
    return (left[0] * right[0] - left[1] * right[1], left[0] * right[1] + left[1] * right[0])


def product_conj(left, right):
    return (left[0] * right[0] + left[1] * right[1], left[1] * right[0] - left[0] * right[1])


def add_pair(left, right):
    return (left[0] + right[0], left[1] + right[1])


def as_matrix(components):
    return [
        [(components[0], components[1]), (components[2], components[3])],
        [(components[4], components[5]), (components[6], components[7])],
    ]


def jones_apply(first, middle, second):
    left_gain = as_matrix(first)
    coherency = as_matrix(middle)
    right_gain = as_matrix(second)
    partial_rows = [
        [
            add_pair(
                product(left_gain[i][0], coherency[0][k]), product(left_gain[i][1], coherency[1][k])
            )
            for k in range(2)
        ]
        for i in range(2)
    ]
    result = []
    for i in range(2):
        for c in range(2):
            element = add_pair(
                product_conj(partial_rows[i][0], right_gain[c][0]),
                product_conj(partial_rows[i][1], right_gain[c][1]),
            )
            result.extend(element)
    return result


def lanes(c):
    return slice(c * 128, (c + 1) * 128)


def calibrate_kernel(gain_ref, left_ref, right_ref, weight_ref, vis_ref, out_ref, gains, gl, gr, cal, wide):
    nb = left_ref.shape[0]
    stations = gain_ref.shape[2]
    for d in range(8):
        for c in range(8):
            gains[d * stations : (d + 1) * stations, lanes(c)] = gain_ref[d, c].astype(F32)
    gains[8 * stations :, :] = jnp.zeros((256 - 8 * stations, 1024), F32)
    table = gains[...].astype(BF16)
    gl[...] = dot(left_ref[...], table)
    gr[...] = dot(right_ref[...], table)

    def step(i, carry):
        rows = pl.ds(pl.multiple_of(i * 16, 16), 16)
        result = jones_apply(
            [gl[rows, lanes(c)] for c in range(8)],
            [vis_ref[c, rows, :].astype(F32) for c in range(8)],
            [gr[rows, lanes(c)] for c in range(8)],
        )
        for c in range(8):
            cal[rows, lanes(c)] = result[c].astype(BF16)
        return carry

    lax.fori_loop(0, nb // 16, step, 0)

    for u in range(UNITS[0]):
        for c in range(8):
            wide[pl.ds(u * 8 + c, 32, ROWS), :] = cal[u * 32 : (u + 1) * 32, lanes(c)].astype(F32)
    for level in (1, 2):
        packed = 1 << level
        width = 128 >> level
        src = iota((128 * packed, 128), 0)
        mean = jnp.where(
            iota((128 * packed, 128), 1) == (src >> 7) * width + ((src & 127) >> level), 1.0 / packed, 0.0
        ).astype(BF16)
        first = BASE[level] * 32
        for g in range(8 // packed):
            cols = slice(g * packed * 128, (g + 1) * packed * 128)
            value = dot(cal[first : first + UNITS[level] * 32, cols], mean)
            for u in range(UNITS[level]):
                row = ROW0[level] + u * (8 // packed) + g
                wide[pl.ds(row, 32, ROWS), :] = value[u * 32 : (u + 1) * 32]
    for m in range(32):
        out_ref[m, 0:ROWS, :] = wide[m * ROWS : (m + 1) * ROWS, :].astype(BF16)

    for level in (1, 2):
        group = iota((256, 256), 0) >> level == iota((256, 256), 1) >> level
        mean = jnp.where(group, 0.5**level, 0.0).astype(BF16)
        rows = slice(BASE[level] * 32, (BASE[level] + UNITS[level]) * 32)
        for c in range(0, 8, 2):
            cols = slice(c * 128, (c + 2) * 128)
            cal[rows, cols] = dot(cal[rows, cols], mean).astype(BF16)
    for c in range(0, 8, 2):
        part = dot(weight_ref[...], cal[:, c * 128 : (c + 2) * 128])
        for m in range(32):
            for half in range(2):
                row = ROWS + (c + half) * 8
                out_ref[m, row : row + 8, :] = part[m * 8 : (m + 1) * 8, lanes(half)].astype(BF16)


def calibrate(gains, left, right, weight, vis):
    nb = left.shape[0]
    vmem = pl.BlockSpec(memory_space=pltpu.VMEM)
    return pl.pallas_call(
        calibrate_kernel,
        in_specs=[vmem] * 5,
        out_specs=vmem,
        out_shape=jax.ShapeDtypeStruct((32, ROWS + 64, 128), BF16),
        scratch_shapes=[
            pltpu.VMEM((256, 1024), F32),
            pltpu.VMEM((nb, 1024), F32),
            pltpu.VMEM((nb, 1024), F32),
            pltpu.VMEM((nb, 1024), BF16),
            pltpu.VMEM((32 * ROWS, 128), F32),
        ],
        compiler_params=pltpu.CompilerParams(vmem_limit_bytes=VMEM_LIMIT),
        name="calibrate",
    )(gains, left, right, weight, vis)


def finish_kernel(recv_ref, pick_ref, lane_ref, time_ref, avg_ref, grid_ref, means):
    for r in range(0, ROWS, 8):
        level = time_ref[r : r + 8, :]
        at_least = [level >= 1.0, level >= 2.0, level >= 3.0]
        for x in range(0, 32, 8):
            value = [recv_ref[x + j, r : r + 8, :].astype(F32) for j in range(8)]
            two = [0.5 * (value[2 * j] + value[2 * j + 1]) for j in range(4)]
            four = [0.5 * (two[2 * j] + two[2 * j + 1]) for j in range(2)]
            eight = 0.5 * (four[0] + four[1])
            top = [jnp.where(at_least[2], eight, four[j]) for j in range(2)]
            mid = [jnp.where(at_least[1], top[j // 2], two[j]) for j in range(4)]
            for j in range(8):
                means[x + j, r : r + 8, :] = jnp.where(at_least[0], mid[j // 2], value[j])

    pick = pick_ref[:, 0:ROWS]
    lane = lane_ref[...]

    def step(i, carry):
        both = jnp.concatenate([means[2 * i], means[2 * i + 1]], axis=1).astype(BF16)
        rows = dot(pick, both)
        for half in range(2):
            value = jnp.take_along_axis(rows[:, lanes(half)], lane, axis=1, mode="promise_in_bounds")
            avg_ref[2 * i + half] = value.astype(BF16).reshape(8, 16, 128)
        return carry

    lax.fori_loop(0, 16, step, 0)

    for c in range(8):
        row = ROWS + c * 8
        total = recv_ref[0, row : row + 8, :].astype(F32)
        for t in range(1, 32):
            total = total + recv_ref[t, row : row + 8, :].astype(F32)
        for u in range(8):
            grid_ref[u, c : c + 1, :] = total[u : u + 1, :]


def finish(recv, pick, lane, time):
    vmem = pl.BlockSpec(memory_space=pltpu.VMEM)
    return pl.pallas_call(
        finish_kernel,
        in_specs=[vmem] * 4,
        out_specs=[vmem] * 2,
        out_shape=[
            jax.ShapeDtypeStruct((32, 8, 16, 128), BF16),
            jax.ShapeDtypeStruct((8, 8, 128), F32),
        ],
        scratch_shapes=[pltpu.VMEM((32, ROWS, 128), F32)],
        compiler_params=pltpu.CompilerParams(vmem_limit_bytes=VMEM_LIMIT),
        name="finish",
    )(recv, pick, lane, time)


def shards(visibilities, station_gains, station_pairs, average_bands, tile_map, baseline_order):
    me = lax.axis_index("tm").reshape(1)
    cut = cut_gains(station_gains)
    gains = lax.all_to_all(cut, "chan", 0, 0, tiled=True)
    moved, left, right, weight, pick, lane, time = prepare(
        me, station_pairs.T, average_bands.T, tile_map.T, baseline_order[None, :], visibilities[0]
    )
    payload = calibrate(gains, left, right, weight, moved)
    recv = lax.all_to_all(payload, "tm", 0, 0, tiled=True)
    averaged, gridded = finish(recv, pick, lane, time)
    return averaged, gridded


def solution(mesh):
    return jax.shard_map(
        shards,
        mesh=mesh,
        in_specs=(P("tm", None, None, "chan"), P(None, "chan", None), P(), P(), P(), P()),
        out_specs=(P(None, None, "tm", "chan"), P("tm", None, "chan")),
        check_vma=False,
    )
```

time: 476 us -> 66 us (0.14)
  waiting for transfers between devices: 275 us -> 6.87 us
  local copies, waits for them, and re-layouts: 142 us -> 1.15 us
  blocking collectives: 0 us -> 41.6 us
  other arithmetic: 31.2 us -> 0 us
  between operations: 14.4 us -> 0.7 us
  Pallas kernels: 0 us -> 10.8 us
  starting transfers between devices: 10.1 us -> 4.47 us
    unnamed x3 -> x0, waiting for transfers between devices: 207 us -> none
    broadcast_in_dim x12 -> x0, local copies, waits for them, and re-layouts: 64.3 us -> none  [the longest x8 47.1 us: halve_time(): return jnp.broadcast_to(merged, shaped.shape).reshape(current.shape)]
    all_gather x1 -> x0, waiting for transfers between devices: 42.4 us -> none  [shards(): all_gains = lax.all_gather(station_gains, 'chan', axis=1, tiled=True)]
    all_to_all x0 -> x1, blocking collectives: none -> 41.6 us  [shards(): recv = lax.all_to_all(payload, 'tm', 0, 0, tiled=True)]
    reshape x3 -> x0, local copies, waits for them, and re-layouts: 30.1 us -> none  [the longest x2 23.9 us: halve_time(): return jnp.broadcast_to(merged, shaped.shape).reshape(current.shape)]
    all_to_all x1, waiting for transfers between devices: 26 us -> 6.87 us  [shards(): gains = lax.all_to_all(cut, 'chan', 0, 0, tiled=True)]
    convert_element_type x2 -> x0, local copies, waits for them, and re-layouts: 15.3 us -> none  [band_average(): values = samples.astype(jnp.float32)]
    unnamed x38 -> x12, local copies, waits for them, and re-layouts: 16.4 us -> 1.15 us
  transfers between devices with their start and end apart: 3 -> 1, of which waited for: 3 -> 1; matrix products, arithmetic and copies ran while one was open for 2% -> 0% of each run, Pallas kernels for 0% -> 3%
where the time goes in v1:
time: 66 us; the launch traced here: 65.6 us
  blocking collectives  41.6 us (63%)
  Pallas kernels  10.8 us (16%)
  waiting for transfers between devices  6.87 us (10%)
  starting transfers between devices  4.47 us (7%)
  local copies, waits for them, and re-layouts  1.15 us (2%)
  between operations  0.7 us (1%)
    all_to_all x1, blocking collectives, shards(): recv = lax.all_to_all(payload, 'tm', 0, 0, tiled=True)  41.6 us
    all_to_all x1, waiting for transfers between devices, shards(): gains = lax.all_to_all(cut, 'chan', 0, 0, tiled=True)  6.87 us
    pallas_call x1, Pallas kernels, finish(): pl.pallas_call(finish_kernel, in_specs=[vmem] * 4, out_specs=[vmem] * 2,...  5.1 us
    all_to_all x1, starting transfers between devices, shards(): gains = lax.all_to_all(cut, 'chan', 0, 0, tiled=True)  4.47 us
    pallas_call x1, Pallas kernels, calibrate(): pl.pallas_call(calibrate_kernel, in_specs=[vmem] * 5, out_specs=vmem, out...  2.91 us
    pallas_call x1, Pallas kernels, prepare(): pl.pallas_call(prepare_kernel, in_specs=[pl.BlockSpec(memory_space=pltpu....  2.02 us
  transfers between devices with their start and end apart: 1, of which 1 were waited for; matrix products, arithmetic and copies ran while one was open for 0% of the time, Pallas kernels for 3%

profile of v1, /device:TPU:32, one launch (start us, length us, event | category | flops | bytes accessed | tf_op | source)
XLA Modules:
  0.0 65.6 jit_solution(5730003121138410189)
XLA Ops:
  0.6 0.0 copy-start
  0.6 1.1 %copy-done = f32[8,24,1024]{2,1,0:T(8,128)S(1)} copy-done((f32[8,24,1024]{2,1,0:T(8,128)S(1)}, f32[8,24,1024]{2,1,0:T(8,128)}, u32[]{:S(2)}) %copy-start) | copy-done | bytes 786456
  1.8 0.0 copy-start.1
  1.8 0.0 copy-start.2
  1.8 0.0 copy-start.3
  1.8 0.0 copy-start.4
  1.8 0.0 copy-start.5
  1.8 0.8 %cut_gains.1 = bf16[8,8,24,128]{3,2,1,0:T(8,128)(2,1)} custom-call(f32[8,24,1024]{2,1,0:T(8,128)S(1)} %copy-done), custom_call_target="tpu_custom_call" | custom-call | tf_op jit(solution)/shard_map/cut_gains/pallas_call | solution.py:49
  2.6 4.5 %all-to-all-start = ((bf16[8,8,24,128]{3,2,1,0:T(8,128)(2,1)}), bf16[8,8,24,128]{3,2,1,0:T(8,128)(2,1)S(1)}, u32[]{:S(2)}, u32[]{:S(2)}) async-start(bf16[8,8,24,128]{3,2,1,0:T(8,128)(2,1)} %cut_gains.1), calls=%async_computation | async-start | bytes 786432 | tf_op jit(solution)/shard_map/all_to_all | solution.py:344
  7.1 0.0 copy-done.1
  7.1 0.0 copy-done.2
  7.1 0.0 copy-done.3
  7.1 0.0 copy-done.4
  7.1 0.0 copy-done.5
  7.1 2.0 %prepare.1 = (bf16[8,512,128]{2,1,0:T(8,128)(2,1)S(1)}, bf16[512,256]{1,0:T(8,128)(2,1)S(1)}, bf16[512,256]{1,0:T(8,128)(2,1)S(1)}, bf16[256,512]{1,0:T(8,128)(2...) custom-call(s32[1]{0:T(128)} %bitcast.me_ref, s32[2,512]{1,0:T(2,128)S(1)} %bitcast.8, ...), custom_call_target="tpu_custom_call" | custom-call | flops 2000000000 | bytes 4000000 | tf_op jit(solution)/shard_map/prepare/pallas_call | solution.py:144
  9.1 6.9 %all-to-all-done.gain_ref = bf16[8,8,24,128]{3,2,1,0:T(8,128)(2,1)S(1)} async-done(((bf16[8,8,24,128]{3,2,1,0:T(8,128)(2,1)}), bf16[8,8,24,128]{3,2,1,0:T(8,128)(2,1)S(1)}, u32[]{:S(2)}, u32[]{:S(2)}) %all-to-all-start) | async-done | bytes 393248 | tf_op jit(solution)/shard_map/all_to_all | solution.py:344
  16.0 2.9 %calibrate.1 = bf16[32,136,128]{2,1,0:T(8,128)(2,1)S(1)} custom-call(bf16[8,8,24,128]{3,2,1,0:T(8,128)(2,1)S(1)} %all-to-all-done.gain_ref, bf16[512,256]{1,0:T(8,128)(2,1)S(1)} %get-tuple-element.9.left_ref, bf16[512,256]{1,0:T(8,128)(2,1)S(1)} %get-tuple-element.10.right_ref, bf16[256,512]{1,0:T(8,128)(2,1)S(1)} %get-tuple-element.11.weight_ref, ...), custom_call_target="tpu_custom_call" | custom-call | tf_op jit(solution)/shard_map/calibrate/pallas_call | solution.py:272
  18.9 41.6 %all_to_all.10.recv_ref = bf16[32,136,128]{2,1,0:T(8,128)(2,1)S(1)} all-to-all(bf16[32,136,128]{2,1,0:T(8,128)(2,1)S(1)} %calibrate.1), channel_id=1, replica_groups=mesh['tm'=32,'chan'=8] {'tm'}, dimensions={0} | all-to-all | bytes 2228224 | tf_op jit(solution)/shard_map/all_to_all | solution.py:349
  60.5 5.1 %finish.1 = (bf16[32,8,16,128]{3,2,1,0:T(8,128)(2,1)}, f32[8,8,128]{2,1,0:T(8,128)}) custom-call(bf16[32,136,128]{2,1,0:T(8,128)(2,1)S(1)} %all_to_all.10.recv_ref, bf16[128,128]{1,0:T(8,128)(2,1)S(1)} %get-tuple-element.13.pick_ref, s32[128,128]{1,0:T(8,128)S(1)} %get-tuple-element.14.lane_ref, f32[128,128]{1,0:T(8,128)S(1)} %get-tuple-element.15.time_ref), custom_call_target="tpu_custom_call" | custom-call | tf_op jit(solution)/shard_map/finish/pallas_call | solution.py:327
Async XLA Ops:
  0.6 1.1 %copy-start = (f32[8,24,1024]{2,1,0:T(8,128)S(1)}, f32[8,24,1024]{2,1,0:T(8,128)}, u32[]{:S(2)}) copy-start(f32[8,24,1024]{2,1,0:T(8,128)} %gain_ref.1) | copy-start | bytes 2359300
  1.8 5.3 %copy-start.1 = (bf16[1,8,512,128]{3,2,1,0:T(8,128)(2,1)S(1)}, bf16[1,8,512,128]{3,2,1,0:T(8,128)(2,1)}, u32[]{:S(2)}) copy-start(bf16[1,8,512,128]{3,2,1,0:T(8,128)(2,1)} %param.6) | copy-start | bytes 3145732
  1.8 5.3 %copy-start.2 = (s32[512,32]{0,1:T(8,128)S(1)}, s32[512,32]{0,1:T(8,128)}, u32[]{:S(2)}) copy-start(s32[512,32]{0,1:T(8,128)} %param.10) | copy-start | bytes 196612
  1.8 5.3 %copy-start.3 = (s32[512,2]{0,1:T(2,128)S(1)}, s32[512,2]{0,1:T(2,128)}, u32[]{:S(2)}) copy-start(s32[512,2]{0,1:T(2,128)} %param.8) | copy-start | bytes 12292
  1.8 5.3 %copy-start.4 = (s32[512,2]{0,1:T(2,128)S(1)}, s32[512,2]{0,1:T(2,128)}, u32[]{:S(2)}) copy-start(s32[512,2]{0,1:T(2,128)} %param.9) | copy-start | bytes 12292
  1.8 5.3 %copy-start.5 = (s32[512]{0:T(512)S(1)}, s32[512]{0:T(512)}, u32[]{:S(2)}) copy-start(s32[512]{0:T(512)} %param.11) | copy-start | bytes 6148
  2.6 13.4 %all-to-all-start = ((bf16[8,8,24,128]{3,2,1,0:T(8,128)(2,1)}), bf16[8,8,24,128]{3,2,1,0:T(8,128)(2,1)S(1)}, u32[]{:S(2)}, u32[]{:S(2)}) async-start(bf16[8,8,24,128]{3,2,1,0:T(8,128)(2,1)} %cut_gains.1), calls=%async_computation | async-start | bytes 786432 | tf_op jit(solution)/shard_map/all_to_all | solution.py:344

commit v2 on v1

--- a/solution.py
+++ b/solution.py
@@ -229,7 +229,7 @@
             cal[rows, lanes(c)] = result[c].astype(BF16)
         return carry
 
-    lax.fori_loop(0, nb // 16, step, 0)
+    lax.fori_loop(0, nb // 16, step, 0, unroll=2)
 
     for u in range(UNITS[0]):
         for c in range(8):
@@ -311,7 +311,7 @@
             avg_ref[2 * i + half] = value.astype(BF16).reshape(8, 16, 128)
         return carry
 
-    lax.fori_loop(0, 16, step, 0)
+    lax.fori_loop(0, 16, step, 0, unroll=8)
 
     for c in range(8):
         row = ROWS + c * 8

time: 66 us -> 63.1 us (0.956)
  Pallas kernels: 10.8 us -> 7.9 us
    pallas_call x1, Pallas kernels: 5.1 us -> 2.28 us  [finish(): pl.pallas_call(finish_kernel, in_specs=[vmem] * 4, out_specs=[vmem] * 2,...]
where the time goes in v2:
time: 63.1 us; the launch traced here: 62.7 us
  blocking collectives  41.6 us (66%)
  Pallas kernels  7.9 us (13%)
  waiting for transfers between devices  6.87 us (11%)
  starting transfers between devices  4.47 us (7%)
  local copies, waits for them, and re-layouts  1.15 us (2%)
  between operations  0.7 us (1%)
    all_to_all x1, blocking collectives, shards(): recv = lax.all_to_all(payload, 'tm', 0, 0, tiled=True)  41.6 us
    all_to_all x1, waiting for transfers between devices, shards(): gains = lax.all_to_all(cut, 'chan', 0, 0, tiled=True)  6.87 us
    all_to_all x1, starting transfers between devices, shards(): gains = lax.all_to_all(cut, 'chan', 0, 0, tiled=True)  4.47 us
    pallas_call x1, Pallas kernels, calibrate(): pl.pallas_call(calibrate_kernel, in_specs=[vmem] * 5, out_specs=vmem, out...  2.8 us
    pallas_call x1, Pallas kernels, finish(): pl.pallas_call(finish_kernel, in_specs=[vmem] * 4, out_specs=[vmem] * 2,...  2.28 us
    pallas_call x1, Pallas kernels, prepare(): pl.pallas_call(prepare_kernel, in_specs=[pl.BlockSpec(memory_space=pltpu....  2.02 us
  transfers between devices with their start and end apart: 1, of which 1 were waited for; matrix products, arithmetic and copies ran while one was open for 0% of the time, Pallas kernels for 3%

profile of v2, /device:TPU:32, one launch (start us, length us, event | category | flops | bytes accessed | tf_op | source)
XLA Modules:
  0.0 62.7 jit_solution(6174055426435960812)
XLA Ops:
  0.6 0.0 copy-start
  0.6 1.1 %copy-done = f32[8,24,1024]{2,1,0:T(8,128)S(1)} copy-done((f32[8,24,1024]{2,1,0:T(8,128)S(1)}, f32[8,24,1024]{2,1,0:T(8,128)}, u32[]{:S(2)}) %copy-start) | copy-done | bytes 786456
  1.8 0.0 copy-start.1
  1.8 0.0 copy-start.2
  1.8 0.0 copy-start.3
  1.8 0.0 copy-start.4
  1.8 0.0 copy-start.5
  1.8 0.8 %cut_gains.1 = bf16[8,8,24,128]{3,2,1,0:T(8,128)(2,1)} custom-call(f32[8,24,1024]{2,1,0:T(8,128)S(1)} %copy-done), custom_call_target="tpu_custom_call" | custom-call | tf_op jit(solution)/shard_map/cut_gains/pallas_call | solution.py:49
  2.6 4.5 %all-to-all-start = ((bf16[8,8,24,128]{3,2,1,0:T(8,128)(2,1)}), bf16[8,8,24,128]{3,2,1,0:T(8,128)(2,1)S(1)}, u32[]{:S(2)}, u32[]{:S(2)}) async-start(bf16[8,8,24,128]{3,2,1,0:T(8,128)(2,1)} %cut_gains.1), calls=%async_computation | async-start | bytes 786432 | tf_op jit(solution)/shard_map/all_to_all | solution.py:344
  7.1 0.0 copy-done.1
  7.1 0.0 copy-done.2
  7.1 0.0 copy-done.3
  7.1 0.0 copy-done.4
  7.1 0.0 copy-done.5
  7.1 2.0 %prepare.1 = (bf16[8,512,128]{2,1,0:T(8,128)(2,1)S(1)}, bf16[512,256]{1,0:T(8,128)(2,1)S(1)}, bf16[512,256]{1,0:T(8,128)(2,1)S(1)}, bf16[256,512]{1,0:T(8,128)(2...) custom-call(s32[1]{0:T(128)} %bitcast.me_ref, s32[2,512]{1,0:T(2,128)S(1)} %bitcast.8, ...), custom_call_target="tpu_custom_call" | custom-call | flops 2000000000 | bytes 4000000 | tf_op jit(solution)/shard_map/prepare/pallas_call | solution.py:144
  9.1 6.9 %all-to-all-done.gain_ref = bf16[8,8,24,128]{3,2,1,0:T(8,128)(2,1)S(1)} async-done(((bf16[8,8,24,128]{3,2,1,0:T(8,128)(2,1)}), bf16[8,8,24,128]{3,2,1,0:T(8,128)(2,1)S(1)}, u32[]{:S(2)}, u32[]{:S(2)}) %all-to-all-start) | async-done | bytes 393248 | tf_op jit(solution)/shard_map/all_to_all | solution.py:344
  16.0 2.8 %calibrate.1 = bf16[32,136,128]{2,1,0:T(8,128)(2,1)S(1)} custom-call(bf16[8,8,24,128]{3,2,1,0:T(8,128)(2,1)S(1)} %all-to-all-done.gain_ref, bf16[512,256]{1,0:T(8,128)(2,1)S(1)} %get-tuple-element.9.left_ref, bf16[512,256]{1,0:T(8,128)(2,1)S(1)} %get-tuple-element.10.right_ref, bf16[256,512]{1,0:T(8,128)(2,1)S(1)} %get-tuple-element.11.weight_ref, ...), custom_call_target="tpu_custom_call" | custom-call | tf_op jit(solution)/shard_map/calibrate/pallas_call | solution.py:272
  18.8 41.6 %all_to_all.10.recv_ref = bf16[32,136,128]{2,1,0:T(8,128)(2,1)S(1)} all-to-all(bf16[32,136,128]{2,1,0:T(8,128)(2,1)S(1)} %calibrate.1), channel_id=1, replica_groups=mesh['tm'=32,'chan'=8] {'tm'}, dimensions={0} | all-to-all | bytes 2228224 | tf_op jit(solution)/shard_map/all_to_all | solution.py:349
  60.4 2.3 %finish.1 = (bf16[32,8,16,128]{3,2,1,0:T(8,128)(2,1)}, f32[8,8,128]{2,1,0:T(8,128)}) custom-call(bf16[32,136,128]{2,1,0:T(8,128)(2,1)S(1)} %all_to_all.10.recv_ref, bf16[128,128]{1,0:T(8,128)(2,1)S(1)} %get-tuple-element.13.pick_ref, s32[128,128]{1,0:T(8,128)S(1)} %get-tuple-element.14.lane_ref, f32[128,128]{1,0:T(8,128)S(1)} %get-tuple-element.15.time_ref), custom_call_target="tpu_custom_call" | custom-call | tf_op jit(solution)/shard_map/finish/pallas_call | solution.py:327
Async XLA Ops:
  0.6 1.1 %copy-start = (f32[8,24,1024]{2,1,0:T(8,128)S(1)}, f32[8,24,1024]{2,1,0:T(8,128)}, u32[]{:S(2)}) copy-start(f32[8,24,1024]{2,1,0:T(8,128)} %gain_ref.1) | copy-start | bytes 2359300
  1.8 5.3 %copy-start.1 = (bf16[1,8,512,128]{3,2,1,0:T(8,128)(2,1)S(1)}, bf16[1,8,512,128]{3,2,1,0:T(8,128)(2,1)}, u32[]{:S(2)}) copy-start(bf16[1,8,512,128]{3,2,1,0:T(8,128)(2,1)} %param.6) | copy-start | bytes 3145732
  1.8 5.3 %copy-start.2 = (s32[512,32]{0,1:T(8,128)S(1)}, s32[512,32]{0,1:T(8,128)}, u32[]{:S(2)}) copy-start(s32[512,32]{0,1:T(8,128)} %param.10) | copy-start | bytes 196612
  1.8 5.3 %copy-start.3 = (s32[512,2]{0,1:T(2,128)S(1)}, s32[512,2]{0,1:T(2,128)}, u32[]{:S(2)}) copy-start(s32[512,2]{0,1:T(2,128)} %param.8) | copy-start | bytes 12292
  1.8 5.3 %copy-start.4 = (s32[512,2]{0,1:T(2,128)S(1)}, s32[512,2]{0,1:T(2,128)}, u32[]{:S(2)}) copy-start(s32[512,2]{0,1:T(2,128)} %param.9) | copy-start | bytes 12292
  1.8 5.3 %copy-start.5 = (s32[512]{0:T(512)S(1)}, s32[512]{0:T(512)}, u32[]{:S(2)}) copy-start(s32[512]{0:T(512)} %param.11) | copy-start | bytes 6148
  2.6 13.4 %all-to-all-start = ((bf16[8,8,24,128]{3,2,1,0:T(8,128)(2,1)}), bf16[8,8,24,128]{3,2,1,0:T(8,128)(2,1)S(1)}, u32[]{:S(2)}, u32[]{:S(2)}) async-start(bf16[8,8,24,128]{3,2,1,0:T(8,128)(2,1)} %cut_gains.1), calls=%async_computation | async-start | bytes 786432 | tf_op jit(solution)/shard_map/all_to_all | solution.py:344

commit v3 on v2

v3 whole, which is shorter than its diff:
```python
import functools
import jax
import jax.numpy as jnp
from jax import lax
from jax.experimental import pallas as pl
from jax.experimental.pallas import tpu as pltpu
from jax.sharding import PartitionSpec as P

KEEP = 320
SEND = 192
FIRST = (0, 96, 192)
SIZES = (96, 96, 128)
UNIT_ROW = (0, 16, 24, 8, 32, 36, 12, 14, 40, 42)
ROWS = 48
MEANS = 80
F32 = jnp.float32
BF16 = jnp.bfloat16
VMEM_LIMIT = 24 << 20


def iota(shape, axis):
    return lax.broadcasted_iota(jnp.int32, shape, axis)


def one_hot(mask):
    return jnp.where(mask, 1.0, 0.0).astype(BF16)


def dot(a, b):
    return lax.dot_general(a, b, (((1,), (0,)), ((), ())), preferred_element_type=F32)


def dot_t(a, b):
    return lax.dot_general(a, b, (((1,), (1,)), ((), ())), preferred_element_type=F32)


def rows_of(values, width):
    row = iota((8, width), 0)
    result = jnp.zeros((8, width), F32)
    for i, value in enumerate(values):
        result = jnp.where(row == i, value, result)
    return result


def gains_kernel(gain_ref, after_ref, out_ref):
    del after_ref
    for d in range(8):
        out_ref[d] = gain_ref[:, :, d * 128 : (d + 1) * 128].astype(BF16)


def cut_gains(gains, after):
    comps, stations, _ = gains.shape
    return pl.pallas_call(
        gains_kernel,
        in_specs=[pl.BlockSpec(memory_space=pltpu.VMEM), pl.BlockSpec(memory_space=pl.ANY)],
        out_shape=jax.ShapeDtypeStruct((8, comps, stations, 128), BF16),
        compiler_params=pltpu.CompilerParams(vmem_limit_bytes=VMEM_LIMIT),
        name="cut_gains",
    )(gains, after)


def route_kernel(me_ref, bands_ref, order_ref, vis_ref, keep_out, send_out, hot_out, position_out):
    me = me_ref[0]
    nb = order_ref.shape[1]
    info = rows_of([bands_ref[0:1, :].astype(F32), bands_ref[1:2, :].astype(F32)], nb).astype(BF16)
    order_hot = one_hot(iota((nb, nb), 0) == order_ref[...])
    at_position = dot(info, order_hot)
    time_here = at_position[0:1, :]
    chan_here = at_position[1:2, :].astype(jnp.int32)
    kind = jnp.where(time_here == 0.0, 0, 3) + chan_here
    same = rows_of([jnp.where(kind == i, 1.0, 0.0) for i in range(6)], nb)
    before = one_hot(
        (iota((nb, nb), 0) < iota((nb, nb), 1)) & ((iota((nb, nb), 0) >> 4) == (iota((nb, nb), 1) >> 4))
    )
    counts = dot(same.astype(BF16), before)
    count = counts[0:1, :]
    for i in range(1, 6):
        count = jnp.where(kind == i, counts[i : i + 1, :], count)
    count = count.astype(jnp.int32)
    side = jnp.where(kind < 3, 0, count >> 1)
    place = jnp.where(kind < 3, count, count & 1)
    kept = jnp.where(chan_here == 0, 1, jnp.where(chan_here == 1, 4, 8)) + place
    sent = 10 + 2 * chan_here + place
    single = jnp.where(chan_here == 0, 0, jnp.where(chan_here == 1, 3, 6)) + place
    unit = jnp.where(kind < 3, single, jnp.where(side == (me & 1), kept, sent))
    slot = unit * 32 + (iota((1, nb), 1) >> 4)
    slot_hot = dot_t(one_hot(iota((nb, nb), 0) == slot), order_hot).astype(BF16)
    for c in range(0, 8, 2):
        both = jnp.concatenate([vis_ref[c], vis_ref[c + 1]], axis=1)
        moved = dot(slot_hot, both).astype(BF16)
        for half in range(2):
            keep_out[c + half] = moved[:KEEP, lanes(half)]
            send_out[c + half] = moved[KEEP:, lanes(half)]
    hot_out[...] = slot_hot[:KEEP]
    position_out[...] = rows_of(
        [time_here, chan_here.astype(F32), kind.astype(F32), side.astype(F32), place.astype(F32)], nb
    )


def route(me, bands, order, vis):
    nb = order.shape[1]
    vmem = pl.BlockSpec(memory_space=pltpu.VMEM)
    return pl.pallas_call(
        route_kernel,
        in_specs=[pl.BlockSpec(memory_space=pltpu.SMEM)] + [vmem] * 3,
        out_shape=[
            jax.ShapeDtypeStruct((8, KEEP, 128), BF16),
            jax.ShapeDtypeStruct((8, SEND, 128), BF16),
            jax.ShapeDtypeStruct((KEEP, nb), BF16),
            jax.ShapeDtypeStruct((8, nb), F32),
        ],
        compiler_params=pltpu.CompilerParams(vmem_limit_bytes=VMEM_LIMIT),
        name="route",
    )(me, bands, order, vis)


def tables_kernel(
    me_ref, pairs_ref, bands_ref, tiles_ref, hot_ref, position_ref,
    left_out, right_out, weight_out, pick_out, lane_out, time_out,
):
    me = me_ref[0]
    nb = pairs_ref.shape[1]
    time_level = bands_ref[0:1, :]
    tile = tiles_ref[pl.ds(me, 1), :]
    for level in range(1, 4):
        start = (me >> level) << level
        tile = jnp.where(time_level == level, tiles_ref[pl.ds(start, 1), :], tile)
    info = rows_of([time_level.astype(F32), tile.astype(F32)], nb).astype(BF16)
    slot_hot = hot_ref[...]
    left_out[...] = dot_t(slot_hot, one_hot(iota((256, nb), 0) == pairs_ref[0:1, :])).astype(BF16)
    right_out[...] = dot_t(slot_hot, one_hot(iota((256, nb), 0) == pairs_ref[1:2, :])).astype(BF16)

    at_slot = dot_t(info, slot_hot)
    time_slot = at_slot[0:1, :]
    weight = jnp.where(time_slot <= 1.0, 1.0, jnp.where(time_slot == 2.0, 0.5, 0.25))
    tile_slot = at_slot[1:2, :].astype(jnp.int32)
    weight_out[...] = jnp.where(iota((256, KEEP), 0) == tile_slot, weight, 0.0).astype(BF16)

    own = dot(
        position_ref[...].astype(BF16), one_hot(iota((nb, 128), 0) == me * 16 + (iota((nb, 128), 1) & 15))
    )
    own_time = own[0:1, :]
    own_chan = own[1:2, :].astype(jnp.int32)
    own_kind = own[2:3, :].astype(jnp.int32)
    own_side = own[3:4, :].astype(jnp.int32)
    own_place = own[4:5, :].astype(jnp.int32)
    comp = iota((1, 128), 1) >> 4
    within = jnp.where(
        own_chan == 0,
        own_place * 8 + comp,
        jnp.where(own_chan == 1, own_place * 4 + (comp >> 1), own_place * 2 + (comp >> 2)),
    )
    single = jnp.where(own_chan == 0, 0, jnp.where(own_chan == 1, 8, 12))
    sided = 16 + 32 * own_side + jnp.where(own_chan == 0, 0, jnp.where(own_chan == 1, 16, 24))
    packed_row = jnp.where(own_kind < 3, single, sided) + within
    part = jnp.where(own_chan == 0, 0, jnp.where(own_chan == 1, 1 + (comp & 1), 3 + (comp & 3)))
    sub = iota((128, 128), 0)
    lan = iota((128, 128), 1)
    eye = one_hot(sub == lan)
    row_hot = one_hot(sub == packed_row)
    pick_out[...] = dot_t(eye, row_hot).astype(BF16)
    part_hot = dot_t(eye, one_hot(sub == part)).astype(BF16)
    table = jnp.where(
        sub == 0,
        lan,
        jnp.where(sub <= 2, (sub - 1) * 64 + (lan >> 1), jnp.where(sub <= 6, (sub - 3) * 32 + (lan >> 2), 0)),
    )
    lane_out[...] = dot(part_hot, table.astype(F32).astype(BF16)).astype(jnp.int32)
    inner = (sub - 16) & 31
    level_of = jnp.where(sub < 8, 0, jnp.where(sub < 12, 1, 2))
    level_of = jnp.where(sub < 16, level_of, jnp.where(inner < 16, 0, jnp.where(inner < 24, 1, 2)))
    share = jnp.where(level_of == 0, 1.0, jnp.where(level_of == 1, 0.5, 0.25))
    spread = jnp.broadcast_to(own_time, (128, 128)).astype(BF16)
    time_out[...] = dot_t(row_hot, spread) * share


def tables(me, pairs, bands, tiles, hot, position):
    vmem = pl.BlockSpec(memory_space=pltpu.VMEM)
    nb = pairs.shape[1]
    return pl.pallas_call(
        tables_kernel,
        in_specs=[pl.BlockSpec(memory_space=pltpu.SMEM)] + [vmem] * 5,
        out_shape=[
            jax.ShapeDtypeStruct((KEEP, 256), BF16),
            jax.ShapeDtypeStruct((KEEP, 256), BF16),
            jax.ShapeDtypeStruct((256, KEEP), BF16),
            jax.ShapeDtypeStruct((128, 128), BF16),
            jax.ShapeDtypeStruct((128, 128), jnp.int32),
            jax.ShapeDtypeStruct((128, 128), F32),
        ],
        compiler_params=pltpu.CompilerParams(vmem_limit_bytes=VMEM_LIMIT),
        cost_estimate=pl.CostEstimate(flops=1_000_000_000, bytes_accessed=4_000_000, transcendentals=0),
        name="tables",
    )(me, pairs, bands, tiles, hot, position)


def product(left, right):
    return (left[0] * right[0] - left[1] * right[1], left[0] * right[1] + left[1] * right[0])


def product_conj(left, right):
    return (left[0] * right[0] + left[1] * right[1], left[1] * right[0] - left[0] * right[1])


def add_pair(left, right):
    return (left[0] + right[0], left[1] + right[1])


def as_matrix(components):
    return [
        [(components[0], components[1]), (components[2], components[3])],
        [(components[4], components[5]), (components[6], components[7])],
    ]


def jones_apply(first, middle, second):
    left_gain = as_matrix(first)
    coherency = as_matrix(middle)
    right_gain = as_matrix(second)
    partial_rows = [
        [
            add_pair(
                product(left_gain[i][0], coherency[0][k]), product(left_gain[i][1], coherency[1][k])
            )
            for k in range(2)
        ]
        for i in range(2)
    ]
    result = []
    for i in range(2):
        for c in range(2):
            element = add_pair(
                product_conj(partial_rows[i][0], right_gain[c][0]),
                product_conj(partial_rows[i][1], right_gain[c][1]),
            )
            result.extend(element)
    return result


def lanes(c):
    return slice(c * 128, (c + 1) * 128)


def calibrate_kernel(gain_ref, left_ref, right_ref, weight_ref, vis_ref, pair_ref, out_ref, gains, gl, gr, cal, wide):
    stations = gain_ref.shape[2]
    for d in range(8):
        for c in range(8):
            gains[d * stations : (d + 1) * stations, lanes(c)] = gain_ref[d, c].astype(F32)
    gains[8 * stations :, :] = jnp.zeros((256 - 8 * stations, 1024), F32)
    table = gains[...].astype(BF16)
    gl[...] = dot(left_ref[...], table)
    gr[...] = dot(right_ref[...], table)

    def block(first, value):
        rows = pl.ds(pl.multiple_of(first, 16), 16)
        result = jones_apply(
            [gl[rows, lanes(c)] for c in range(8)],
            [value(c, rows) for c in range(8)],
            [gr[rows, lanes(c)] for c in range(8)],
        )
        for c in range(8):
            cal[rows, lanes(c)] = result[c].astype(BF16)

    for level, singles in ((0, 32), (1, 32), (2, 64)):

        def single(i, carry, level=level):
            block(FIRST[level] + i * 16, lambda c, rows: vis_ref[c, rows, :].astype(F32))
            return carry

        def paired(i, carry, level=level, singles=singles):
            other = pl.ds(pl.multiple_of(level * 64 + i * 16, 16), 16)
            block(
                FIRST[level] + singles + i * 16,
                lambda c, rows: 0.5 * (vis_ref[c, rows, :].astype(F32) + pair_ref[c, other, :].astype(F32)),
            )
            return carry

        lax.fori_loop(0, singles // 16, single, 0, unroll=2)
        lax.fori_loop(0, 4, paired, 0, unroll=2)

    for u in range(3):
        for c in range(8):
            wide[pl.ds(UNIT_ROW[u] + c, 32, ROWS), :] = cal[u * 32 : (u + 1) * 32, lanes(c)].astype(F32)
    for level in (1, 2):
        packed = 1 << level
        width = 128 >> level
        src = iota((128 * packed, 128), 0)
        mean = jnp.where(
            iota((128 * packed, 128), 1) == (src >> 7) * width + ((src & 127) >> level), 1.0 / packed, 0.0
        ).astype(BF16)
        first = FIRST[level]
        for g in range(8 // packed):
            cols = slice(g * packed * 128, (g + 1) * packed * 128)
            value = dot(cal[first : first + SIZES[level], cols], mean)
            for u in range(SIZES[level] // 32):
                row = UNIT_ROW[first // 32 + u] + g
                wide[pl.ds(row, 32, ROWS), :] = value[u * 32 : (u + 1) * 32]
    for row in range(44, ROWS):
        wide[pl.ds(row, 32, ROWS), :] = jnp.zeros((32, 128), F32)
    for m in range(32):
        out_ref[m, 0:ROWS, :] = wide[m * ROWS : (m + 1) * ROWS, :].astype(BF16)

    for level in (1, 2):
        group = iota((256, 256), 0) >> level == iota((256, 256), 1) >> level
        mean = jnp.where(group, 0.5**level, 0.0).astype(BF16)
        rows = slice(FIRST[level], FIRST[level] + SIZES[level])
        for c in range(0, 8, 2):
            cols = slice(c * 128, (c + 2) * 128)
            cal[rows, cols] = dot(cal[rows, cols], mean).astype(BF16)
    for c in range(0, 8, 2):
        part = dot(weight_ref[...], cal[:, c * 128 : (c + 2) * 128])
        for m in range(32):
            for half in range(2):
                row = ROWS + (c + half) * 8
                out_ref[m, row : row + 8, :] = part[m * 8 : (m + 1) * 8, lanes(half)].astype(BF16)


def calibrate(gains, left, right, weight, vis, pair):
    vmem = pl.BlockSpec(memory_space=pltpu.VMEM)
    return pl.pallas_call(
        calibrate_kernel,
        in_specs=[vmem] * 6,
        out_specs=vmem,
        out_shape=jax.ShapeDtypeStruct((32, ROWS + 64, 128), BF16),
        scratch_shapes=[
            pltpu.VMEM((256, 1024), F32),
            pltpu.VMEM((KEEP, 1024), F32),
            pltpu.VMEM((KEEP, 1024), F32),
            pltpu.VMEM((KEEP, 1024), BF16),
            pltpu.VMEM((32 * ROWS, 128), F32),
        ],
        compiler_params=pltpu.CompilerParams(vmem_limit_bytes=VMEM_LIMIT),
        name="calibrate",
    )(gains, left, right, weight, vis, pair)


def finish_kernel(recv_ref, pick_ref, lane_ref, time_ref, avg_ref, grid_ref, means):
    for t in range(32):
        means[t, 0:16, :] = recv_ref[t, 0:16, :].astype(F32)
    for side in range(2):
        for r in range(16, ROWS, 8):
            row = r + 32 * side
            level = time_ref[row : row + 8, :]
            at_least = [level >= 2.0, level >= 3.0]
            for x in range(0, 32, 8):
                two = [recv_ref[x + 2 * j + side, r : r + 8, :].astype(F32) for j in range(4)]
                four = [0.5 * (two[2 * j] + two[2 * j + 1]) for j in range(2)]
                eight = 0.5 * (four[0] + four[1])
                top = [jnp.where(at_least[1], eight, four[j]) for j in range(2)]
                for j in range(4):
                    value = jnp.where(at_least[0], top[j // 2], two[j])
                    means[x + 2 * j, row : row + 8, :] = value
                    means[x + 2 * j + 1, row : row + 8, :] = value

    pick = pick_ref[:, 0:MEANS]
    lane = lane_ref[...]

    def step(i, carry):
        both = jnp.concatenate([means[2 * i], means[2 * i + 1]], axis=1).astype(BF16)
        rows = dot(pick, both)
        for half in range(2):
            value = jnp.take_along_axis(rows[:, lanes(half)], lane, axis=1, mode="promise_in_bounds")
            avg_ref[2 * i + half] = value.astype(BF16).reshape(8, 16, 128)
        return carry

    lax.fori_loop(0, 16, step, 0, unroll=8)

    for c in range(8):
        row = ROWS + c * 8
        total = recv_ref[0, row : row + 8, :].astype(F32)
        for t in range(1, 32):
            total = total + recv_ref[t, row : row + 8, :].astype(F32)
        for u in range(8):
            grid_ref[u, c : c + 1, :] = total[u : u + 1, :]


def finish(recv, pick, lane, time):
    vmem = pl.BlockSpec(memory_space=pltpu.VMEM)
    return pl.pallas_call(
        finish_kernel,
        in_specs=[vmem] * 4,
        out_specs=[vmem] * 2,
        out_shape=[
            jax.ShapeDtypeStruct((32, 8, 16, 128), BF16),
            jax.ShapeDtypeStruct((8, 8, 128), F32),
        ],
        scratch_shapes=[pltpu.VMEM((32, MEANS, 128), F32)],
        compiler_params=pltpu.CompilerParams(vmem_limit_bytes=VMEM_LIMIT),
        name="finish",
    )(recv, pick, lane, time)


def shards(visibilities, station_gains, station_pairs, average_bands, tile_map, baseline_order):
    me = lax.axis_index("tm").reshape(1)
    bands = average_bands.T
    keep, send, hot, position = route(me, bands, baseline_order[None, :], visibilities[0])
    pair = lax.ppermute(send, "tm", [(m, m ^ 1) for m in range(32)])
    gains = lax.all_to_all(cut_gains(station_gains, position), "chan", 0, 0, tiled=True)
    left, right, weight, pick, lane, time = tables(me, station_pairs.T, bands, tile_map.T, hot, position)
    payload = calibrate(gains, left, right, weight, keep, pair)
    recv = lax.all_to_all(payload, "tm", 0, 0, tiled=True)
    averaged, gridded = finish(recv, pick, lane, time)
    return averaged, gridded


def solution(mesh):
    return jax.shard_map(
        shards,
        mesh=mesh,
        in_specs=(P("tm", None, None, "chan"), P(None, "chan", None), P(), P(), P(), P()),
        out_specs=(P(None, None, "tm", "chan"), P("tm", None, "chan")),
        check_vma=False,
    )
```

time: 63.1 us -> 60.9 us (0.965)
  blocking collectives: 41.6 us -> 36.9 us
  local copies, waits for them, and re-layouts: 1.15 us -> 2.59 us
  starting transfers between devices: 4.47 us -> 5.51 us
    all_to_all x1, blocking collectives: 41.6 us -> 36.9 us  [shards(): recv = lax.all_to_all(payload, 'tm', 0, 0, tiled=True)]
    ppermute x0 -> x1, starting transfers between devices: none -> 1.93 us  [shards(): pair = lax.ppermute(send, 'tm', [(m, m ^ 1) for m in range(32)])]
    unnamed x12, local copies, waits for them, and re-layouts: 1.15 us -> 2.59 us
    all_to_all x1, starting transfers between devices: 4.47 us -> 3.58 us  [shards(): lax.all_to_all(cut_gains(station_gains, position), 'chan', 0, 0, tiled=True)]
    pallas_call x3 -> x4, Pallas kernels: 5.62 us -> 5.22 us  [the longest x1 2.32 us: calibrate(): pl.pallas_call(calibrate_kernel, in_specs=[vmem] * 6, out_specs=vmem, out...]
  transfers between devices with their start and end apart: 1 -> 2, of which waited for: 1 -> 1; matrix products, arithmetic and copies ran while one was open for 0% -> 0% of each run, Pallas kernels for 3% -> 3%
where the time goes in v3:
time: 60.9 us; the launch traced here: 60.5 us
  blocking collectives  36.9 us (61%)
  waiting for transfers between devices  7.43 us (12%)
  Pallas kernels  7.39 us (12%)
  starting transfers between devices  5.51 us (9%)
  local copies, waits for them, and re-layouts  2.59 us (4%)
  between operations  0.7 us (1%)
    all_to_all x1, blocking collectives, shards(): recv = lax.all_to_all(payload, 'tm', 0, 0, tiled=True)  36.9 us
    all_to_all x1, waiting for transfers between devices, shards(): lax.all_to_all(cut_gains(station_gains, position), 'chan', 0, 0, tiled=True)  7.43 us
    all_to_all x1, starting transfers between devices, shards(): lax.all_to_all(cut_gains(station_gains, position), 'chan', 0, 0, tiled=True)  3.58 us
    unnamed x12, local copies, waits for them, and re-layouts  2.59 us
    pallas_call x1, Pallas kernels, calibrate(): pl.pallas_call(calibrate_kernel, in_specs=[vmem] * 6, out_specs=vmem, out...  2.32 us
    pallas_call x1, Pallas kernels, finish(): pl.pallas_call(finish_kernel, in_specs=[vmem] * 4, out_specs=[vmem] * 2,...  2.17 us
    ppermute x1, starting transfers between devices, shards(): pair = lax.ppermute(send, 'tm', [(m, m ^ 1) for m in range(32)])  1.93 us
    pallas_call x1, Pallas kernels, route(): pl.pallas_call(route_kernel, in_specs=[pl.BlockSpec(memory_space=pltpu.SM...  1.38 us
  transfers between devices with their start and end apart: 2, of which 1 were waited for; matrix products, arithmetic and copies ran while one was open for 0% of the time, Pallas kernels for 3%

profile of v3, /device:TPU:32, one launch (start us, length us, event | category | flops | bytes accessed | tf_op | source)
XLA Modules:
  0.0 60.5 jit_solution(6019027447612173402)
XLA Ops:
  0.6 0.0 copy-start.2
  0.6 0.0 copy-start.3
  0.7 0.7 %copy-done.2 = s32[512,2]{0,1:T(2,128)S(1)} copy-done((s32[512,2]{0,1:T(2,128)S(1)}, s32[512,2]{0,1:T(2,128)}, u32[]{:S(2)}) %copy-start.2) | copy-done | bytes 4120
  1.3 0.0 copy-done.3
  1.3 0.0 copy-start
  1.3 1.2 %copy-done = bf16[1,8,512,128]{3,2,1,0:T(8,128)(2,1)S(1)} copy-done((bf16[1,8,512,128]{3,2,1,0:T(8,128)(2,1)S(1)}, bf16[1,8,512,128]{3,2,1,0:T(8,128)(2,1)}, u32[]{:S(2)}) %copy-start) | copy-done | bytes 1048600
  2.6 0.0 copy-start.1
  2.6 1.4 %route.1 = (bf16[8,320,128]{2,1,0:T(8,128)(2,1)S(1)}, bf16[8,192,128]{2,1,0:T(8,128)(2,1)S(1)}, bf16[320,512]{1,0:T(8,128)(2,1)S(1)}, f32[8,512]{1,0:T(8,128)S(1)}) custom-call(s32[1]{0:T(128)} %bitcast.me_ref, s32[2,512]{1,0:T(2,128)S(1)} %bitcast.7, s32[1,512]{1,0:T(1,128)S(1)} %bitcast.9, bf16[8,512,128]{2,1,0:T(8,128)(2,1)S(1)} %bitcast.6), custom_call_target="tpu_custom_call" | custom-call | tf_op jit(solution)/shard_map/route/pallas_call | solution.py:103
  3.9 1.9 %collective-permute-start = (bf16[8,192,128]{2,1,0:T(8,128)(2,1)S(1)}, bf16[8,192,128]{2,1,0:T(8,128)(2,1)S(1)}, u32[]{:S(2)}, u32[]{:S(2)}) collective-permute-start(bf16[8,192,128]{2,1,0:T(8,128)(2,1)S(1)} %get-tuple-element.18), channel_id=1, source_target_pairs={{0,8},{8,0},{16,24},{24,16},{32,40},{40,32},{48,56},{56,48},{64,72... | collective-permute-start | bytes 1179656 | tf_op jit(solution)/shard_map/ppermute | solution.py:397
  5.9 0.0 copy-done.1
  5.9 0.8 %cut_gains.1 = bf16[8,8,24,128]{3,2,1,0:T(8,128)(2,1)} custom-call(f32[8,24,1024]{2,1,0:T(8,128)S(1)} %copy-done.1, f32[8,512]{1,0:T(8,128)S(1)} %get-tuple-element.12.after_ref.position_ref), custom_call_target="tpu_custom_call" | custom-call | tf_op jit(solution)/shard_map/cut_gains/pallas_call | solution.py:53
  6.7 0.0 copy-start.4
  6.7 3.6 %all-to-all-start = ((bf16[8,8,24,128]{3,2,1,0:T(8,128)(2,1)}), bf16[8,8,24,128]{3,2,1,0:T(8,128)(2,1)S(1)}, u32[]{:S(2)}, u32[]{:S(2)}) async-start(bf16[8,8,24,128]{3,2,1,0:T(8,128)(2,1)} %cut_gains.1), calls=%async_computation | async-start | bytes 786432 | tf_op jit(solution)/shard_map/all_to_all | solution.py:398
  10.3 0.0 copy-start.5
  10.3 0.0 copy-done.4
  10.3 0.7 %copy-done.5 = s32[512,2]{0,1:T(2,128)S(1)} copy-done((s32[512,2]{0,1:T(2,128)S(1)}, s32[512,2]{0,1:T(2,128)}, u32[]{:S(2)}) %copy-start.5) | copy-done | bytes 4120
  11.0 0.7 %tables.1 = (bf16[320,256]{1,0:T(8,128)(2,1)S(1)}, bf16[320,256]{1,0:T(8,128)(2,1)S(1)}, bf16[256,320]{1,0:T(8,128)(2,1)S(1)}, bf16[128,128]{1,0:T(8,128)(2,1)S(...) custom-call(s32[1]{0:T(128)} %bitcast.me_ref, s32[2,512]{1,0:T(2,128)S(1)} %bitcast.11, s32[2,512]{1,0:T(2,128)S(1)} %bitcast.8, ...), custom_call_target="tpu_custom_call" | custom-call | flops 1000000000 | bytes 4000000 | tf_op jit(solution)/shard_map/tables/pallas_call | solution.py:180
  11.7 7.4 %all-to-all-done.gain_ref = bf16[8,8,24,128]{3,2,1,0:T(8,128)(2,1)S(1)} async-done(((bf16[8,8,24,128]{3,2,1,0:T(8,128)(2,1)}), bf16[8,8,24,128]{3,2,1,0:T(8,128)(2,1)S(1)}, u32[]{:S(2)}, u32[]{:S(2)}) %all-to-all-start) | async-done | bytes 393248 | tf_op jit(solution)/shard_map/all_to_all | solution.py:398
  19.1 0.0 collective-permute-done.pair_ref
  19.1 2.3 %calibrate.1 = bf16[32,112,128]{2,1,0:T(8,128)(2,1)S(1)} custom-call(bf16[8,8,24,128]{3,2,1,0:T(8,128)(2,1)S(1)} %all-to-all-done.gain_ref, bf16[320,256]{1,0:T(8,128)(2,1)S(1)} %get-tuple-element.14.left_ref, bf16[320,256]{1,0:T(8,128)(2,1)S(1)} %get-tuple-element.15.right_ref, bf16[256,320]{1,0:T(8,128)(2,1)S(1)} %get-tuple-element.16.weight_ref, ...), custom_call_target="tpu_custom_call" | custom-call | tf_op jit(solution)/shard_map/calibrate/pallas_call | solution.py:320
  21.5 36.9 %all_to_all.10.recv_ref = bf16[32,112,128]{2,1,0:T(8,128)(2,1)S(1)} all-to-all(bf16[32,112,128]{2,1,0:T(8,128)(2,1)S(1)} %calibrate.1), channel_id=1, replica_groups=mesh['tm'=32,'chan'=8] {'tm'}, dimensions={0} | all-to-all | bytes 1835008 | tf_op jit(solution)/shard_map/all_to_all | solution.py:401
  58.4 2.2 %finish.1 = (bf16[32,8,16,128]{3,2,1,0:T(8,128)(2,1)}, f32[8,8,128]{2,1,0:T(8,128)}) custom-call(bf16[32,112,128]{2,1,0:T(8,128)(2,1)S(1)} %all_to_all.10.recv_ref, bf16[128,128]{1,0:T(8,128)(2,1)S(1)} %get-tuple-element.19.pick_ref, s32[128,128]{1,0:T(8,128)S(1)} %get-tuple-element.20.lane_ref, f32[128,128]{1,0:T(8,128)S(1)} %get-tuple-element.21.time_ref), custom_call_target="tpu_custom_call" | custom-call | tf_op jit(solution)/shard_map/finish/pallas_call | solution.py:379
Async XLA Ops:
  0.6 0.7 %copy-start.2 = (s32[512,2]{0,1:T(2,128)S(1)}, s32[512,2]{0,1:T(2,128)}, u32[]{:S(2)}) copy-start(s32[512,2]{0,1:T(2,128)} %param.9) | copy-start | bytes 12292
  0.6 0.7 %copy-start.3 = (s32[512]{0:T(512)S(1)}, s32[512]{0:T(512)}, u32[]{:S(2)}) copy-start(s32[512]{0:T(512)} %param.11) | copy-start | bytes 6148
  1.3 1.2 %copy-start = (bf16[1,8,512,128]{3,2,1,0:T(8,128)(2,1)S(1)}, bf16[1,8,512,128]{3,2,1,0:T(8,128)(2,1)}, u32[]{:S(2)}) copy-start(bf16[1,8,512,128]{3,2,1,0:T(8,128)(2,1)} %param.6) | copy-start | bytes 3145732
  2.6 3.3 %copy-start.1 = (f32[8,24,1024]{2,1,0:T(8,128)S(1)}, f32[8,24,1024]{2,1,0:T(8,128)}, u32[]{:S(2)}) copy-start(f32[8,24,1024]{2,1,0:T(8,128)} %gain_ref.1) | copy-start | bytes 2359300
  3.9 15.2 %collective-permute-start = (bf16[8,192,128]{2,1,0:T(8,128)(2,1)S(1)}, bf16[8,192,128]{2,1,0:T(8,128)(2,1)S(1)}, u32[]{:S(2)}, u32[]{:S(2)}) collective-permute-start(bf16[8,192,128]{2,1,0:T(8,128)(2,1)S(1)} %get-tuple-element.18), channel_id=1, source_target_pairs={{0,8},{8,0},{16,24},{24,16},{32,40},{40,32},{48,56},{56,48},{64,72... | collective-permute-start | bytes 1179656 | tf_op jit(solution)/shard_map/ppermute | solution.py:397
  6.7 3.6 %copy-start.4 = (s32[512,32]{0,1:T(8,128)S(1)}, s32[512,32]{0,1:T(8,128)}, u32[]{:S(2)}) copy-start(s32[512,32]{0,1:T(8,128)} %param.10) | copy-start | bytes 196612
  6.7 12.5 %all-to-all-start = ((bf16[8,8,24,128]{3,2,1,0:T(8,128)(2,1)}), bf16[8,8,24,128]{3,2,1,0:T(8,128)(2,1)S(1)}, u32[]{:S(2)}, u32[]{:S(2)}) async-start(bf16[8,8,24,128]{3,2,1,0:T(8,128)(2,1)} %cut_gains.1), calls=%async_computation | async-start | bytes 786432 | tf_op jit(solution)/shard_map/all_to_all | solution.py:398
  10.3 0.7 %copy-start.5 = (s32[512,2]{0,1:T(2,128)S(1)}, s32[512,2]{0,1:T(2,128)}, u32[]{:S(2)}) copy-start(s32[512,2]{0,1:T(2,128)} %param.8) | copy-start | bytes 12292

commit v4 on v3

--- a/solution.py
+++ b/solution.py
@@ -34,6 +34,14 @@
     return lax.dot_general(a, b, (((1,), (1,)), ((), ())), preferred_element_type=F32)
 
 
+def roll64(value):
+    return pltpu.roll(value, 64, 1)
+
+
+def low_lanes(rows):
+    return iota((rows, 128), 1) < 64
+
+
 def rows_of(values, width):
     row = iota((8, width), 0)
     result = jnp.zeros((8, width), F32)
@@ -42,24 +50,36 @@
     return result
 
 
-def gains_kernel(gain_ref, after_ref, out_ref):
+def gains_kernel(me_ref, gain_ref, after_ref, out_ref):
     del after_ref
+    first_half = ((me_ref[0] >> 3) & 1) == 0
+    stations = gain_ref.shape[1]
+    low = low_lanes(stations)
     for d in range(8):
-        out_ref[d] = gain_ref[:, :, d * 128 : (d + 1) * 128].astype(BF16)
-
-
-def cut_gains(gains, after):
+        for g in range(4):
+            a = gain_ref[2 * g, :, d * 128 : (d + 1) * 128]
+            b = gain_ref[2 * g + 1, :, d * 128 : (d + 1) * 128]
+            a = jnp.where(first_half, a, roll64(a))
+            b = jnp.where(first_half, roll64(b), b)
+            out_ref[d, g * stations : (g + 1) * stations, :] = jnp.where(low, a, b).astype(BF16)
+
+
+def cut_gains(me, gains, after):
     comps, stations, _ = gains.shape
     return pl.pallas_call(
         gains_kernel,
-        in_specs=[pl.BlockSpec(memory_space=pltpu.VMEM), pl.BlockSpec(memory_space=pl.ANY)],
-        out_shape=jax.ShapeDtypeStruct((8, comps, stations, 128), BF16),
+        in_specs=[
+            pl.BlockSpec(memory_space=pltpu.SMEM),
+            pl.BlockSpec(memory_space=pltpu.VMEM),
+            pl.BlockSpec(memory_space=pl.ANY),
+        ],
+        out_shape=jax.ShapeDtypeStruct((8, comps // 2 * stations, 128), BF16),
         compiler_params=pltpu.CompilerParams(vmem_limit_bytes=VMEM_LIMIT),
         name="cut_gains",
-    )(gains, after)
-
-
-def route_kernel(me_ref, bands_ref, order_ref, vis_ref, keep_out, send_out, hot_out, position_out):
+    )(me, gains, after)
+
+
+def route_kernel(me_ref, bands_ref, order_ref, vis_ref, keep_out, x_out, z_out, xz_out, hot_out, position_out):
     me = me_ref[0]
     nb = order_ref.shape[1]
     info = rows_of([bands_ref[0:1, :].astype(F32), bands_ref[1:2, :].astype(F32)], nb).astype(BF16)
@@ -85,12 +105,22 @@
     unit = jnp.where(kind < 3, single, jnp.where(side == (me & 1), kept, sent))
     slot = unit * 32 + (iota((1, nb), 1) >> 4)
     slot_hot = dot_t(one_hot(iota((nb, nb), 0) == slot), order_hot).astype(BF16)
-    for c in range(0, 8, 2):
-        both = jnp.concatenate([vis_ref[c], vis_ref[c + 1]], axis=1)
-        moved = dot(slot_hot, both).astype(BF16)
-        for half in range(2):
-            keep_out[c + half] = moved[:KEEP, lanes(half)]
-            send_out[c + half] = moved[KEEP:, lanes(half)]
+    first_half = ((me >> 3) & 1) == 0
+    low = low_lanes(nb)
+    for g in range(4):
+        both = jnp.concatenate([vis_ref[2 * g], vis_ref[2 * g + 1]], axis=1)
+        moved = dot(slot_hot, both)
+        a = moved[:, lanes(0)]
+        b = moved[:, lanes(1)]
+        keep_out[2 * g] = a[:KEEP].astype(BF16)
+        keep_out[2 * g + 1] = b[:KEEP].astype(BF16)
+        lower = jnp.where(low, a, roll64(b))
+        upper = jnp.where(low, roll64(a), b)
+        here = jnp.where(first_half, lower, upper).astype(BF16)
+        there = jnp.where(first_half, upper, lower).astype(BF16)
+        x_out[g] = there[:KEEP]
+        xz_out[g] = there[KEEP:]
+        z_out[g] = here[KEEP:]
     hot_out[...] = slot_hot[:KEEP]
     position_out[...] = rows_of(
         [time_here, chan_here.astype(F32), kind.astype(F32), side.astype(F32), place.astype(F32)], nb
@@ -105,7 +135,9 @@
         in_specs=[pl.BlockSpec(memory_space=pltpu.SMEM)] + [vmem] * 3,
         out_shape=[
             jax.ShapeDtypeStruct((8, KEEP, 128), BF16),
-            jax.ShapeDtypeStruct((8, SEND, 128), BF16),
+            jax.ShapeDtypeStruct((4, KEEP, 128), BF16),
+            jax.ShapeDtypeStruct((4, SEND, 128), BF16),
+            jax.ShapeDtypeStruct((4, SEND, 128), BF16),
             jax.ShapeDtypeStruct((KEEP, nb), BF16),
             jax.ShapeDtypeStruct((8, nb), F32),
         ],
@@ -121,11 +153,14 @@
     me = me_ref[0]
     nb = pairs_ref.shape[1]
     time_level = bands_ref[0:1, :]
-    tile = tiles_ref[pl.ds(me, 1), :]
-    for level in range(1, 4):
-        start = (me >> level) << level
-        tile = jnp.where(time_level == level, tiles_ref[pl.ds(start, 1), :], tile)
-    info = rows_of([time_level.astype(F32), tile.astype(F32)], nb).astype(BF16)
+    tiles = []
+    for now in (me & ~8, me | 8):
+        tile = tiles_ref[pl.ds(now, 1), :]
+        for level in range(1, 4):
+            start = (now >> level) << level
+            tile = jnp.where(time_level == level, tiles_ref[pl.ds(start, 1), :], tile)
+        tiles.append(tile.astype(F32))
+    info = rows_of([time_level.astype(F32)] + tiles, nb).astype(BF16)
     slot_hot = hot_ref[...]
     left_out[...] = dot_t(slot_hot, one_hot(iota((256, nb), 0) == pairs_ref[0:1, :])).astype(BF16)
     right_out[...] = dot_t(slot_hot, one_hot(iota((256, nb), 0) == pairs_ref[1:2, :])).astype(BF16)
@@ -133,8 +168,9 @@
     at_slot = dot_t(info, slot_hot)
     time_slot = at_slot[0:1, :]
     weight = jnp.where(time_slot <= 1.0, 1.0, jnp.where(time_slot == 2.0, 0.5, 0.25))
-    tile_slot = at_slot[1:2, :].astype(jnp.int32)
-    weight_out[...] = jnp.where(iota((256, KEEP), 0) == tile_slot, weight, 0.0).astype(BF16)
+    for i in range(2):
+        tile_slot = at_slot[1 + i : 2 + i, :].astype(jnp.int32)
+        weight_out[i] = jnp.where(iota((256, KEEP), 0) == tile_slot, weight, 0.0).astype(BF16)
 
     own = dot(
         position_ref[...].astype(BF16), one_hot(iota((nb, 128), 0) == me * 16 + (iota((nb, 128), 1) & 15))
@@ -160,12 +196,18 @@
     row_hot = one_hot(sub == packed_row)
     pick_out[...] = dot_t(eye, row_hot).astype(BF16)
     part_hot = dot_t(eye, one_hot(sub == part)).astype(BF16)
-    table = jnp.where(
-        sub == 0,
-        lan,
-        jnp.where(sub <= 2, (sub - 1) * 64 + (lan >> 1), jnp.where(sub <= 6, (sub - 3) * 32 + (lan >> 2), 0)),
-    )
-    lane_out[...] = dot(part_hot, table.astype(F32).astype(BF16)).astype(jnp.int32)
+    inside = lan & 63
+    for bit in range(2):
+        table = jnp.where(
+            sub == 0,
+            bit * 64 + inside,
+            jnp.where(
+                sub <= 2,
+                (sub - 1) * 64 + bit * 32 + (inside >> 1),
+                jnp.where(sub <= 6, (sub - 3) * 32 + bit * 16 + (inside >> 2), 0),
+            ),
+        )
+        lane_out[bit] = dot(part_hot, table.astype(F32).astype(BF16)).astype(jnp.int32)
     inner = (sub - 16) & 31
     level_of = jnp.where(sub < 8, 0, jnp.where(sub < 12, 1, 2))
     level_of = jnp.where(sub < 16, level_of, jnp.where(inner < 16, 0, jnp.where(inner < 24, 1, 2)))
@@ -183,9 +225,9 @@
         out_shape=[
             jax.ShapeDtypeStruct((KEEP, 256), BF16),
             jax.ShapeDtypeStruct((KEEP, 256), BF16),
-            jax.ShapeDtypeStruct((256, KEEP), BF16),
+            jax.ShapeDtypeStruct((2, 256, KEEP), BF16),
             jax.ShapeDtypeStruct((128, 128), BF16),
-            jax.ShapeDtypeStruct((128, 128), jnp.int32),
+            jax.ShapeDtypeStruct((2, 128, 128), jnp.int32),
             jax.ShapeDtypeStruct((128, 128), F32),
         ],
         compiler_params=pltpu.CompilerParams(vmem_limit_bytes=VMEM_LIMIT),
@@ -241,22 +283,43 @@
     return slice(c * 128, (c + 1) * 128)
 
 
-def calibrate_kernel(gain_ref, left_ref, right_ref, weight_ref, vis_ref, pair_ref, out_ref, gains, gl, gr, cal, wide):
-    stations = gain_ref.shape[2]
+def calibrate_kernel(
+    me_ref, gain_ref, left_ref, right_ref, weight_ref, vis_ref, x_ref, z_ref, xz_ref, out_ref, gains, gl, gr, cal, wide
+):
+    stations = gain_ref.shape[1] // 4
+    low = low_lanes(stations)
     for d in range(8):
-        for c in range(8):
-            gains[d * stations : (d + 1) * stations, lanes(c)] = gain_ref[d, c].astype(F32)
+        for g in range(4):
+            both = gain_ref[d, g * stations : (g + 1) * stations, :].astype(F32)
+            swapped = roll64(both)
+            gains[d * stations : (d + 1) * stations, lanes(2 * g)] = jnp.where(low, both, swapped)
+            gains[d * stations : (d + 1) * stations, lanes(2 * g + 1)] = jnp.where(low, swapped, both)
     gains[8 * stations :, :] = jnp.zeros((256 - 8 * stations, 1024), F32)
     table = gains[...].astype(BF16)
     gl[...] = dot(left_ref[...], table)
     gr[...] = dot(right_ref[...], table)
 
-    def block(first, value):
+    first_half = ((me_ref[0] >> 3) & 1) == 0
+    mine = low_lanes(16) == first_half
+
+    def spread(ref, g, rows, front):
+        both = ref[g, rows, :].astype(F32)
+        swapped = roll64(both)
+        return jnp.where(front, both, swapped), jnp.where(front, swapped, both)
+
+    def block(first, other):
         rows = pl.ds(pl.multiple_of(first, 16), 16)
+        value = []
+        for g in range(4):
+            theirs = spread(x_ref, g, rows, jnp.logical_not(first_half))
+            pair = [jnp.where(mine, vis_ref[2 * g + i, rows, :].astype(F32), theirs[i]) for i in range(2)]
+            if other is not None:
+                near = spread(z_ref, g, other, first_half)
+                far = spread(xz_ref, g, other, jnp.logical_not(first_half))
+                pair = [0.5 * (pair[i] + jnp.where(mine, near[i], far[i])) for i in range(2)]
+            value.extend(pair)
         result = jones_apply(
-            [gl[rows, lanes(c)] for c in range(8)],
-            [value(c, rows) for c in range(8)],
-            [gr[rows, lanes(c)] for c in range(8)],
+            [gl[rows, lanes(c)] for c in range(8)], value, [gr[rows, lanes(c)] for c in range(8)]
         )
         for c in range(8):
             cal[rows, lanes(c)] = result[c].astype(BF16)
@@ -264,15 +327,12 @@
     for level, singles in ((0, 32), (1, 32), (2, 64)):
 
         def single(i, carry, level=level):
-            block(FIRST[level] + i * 16, lambda c, rows: vis_ref[c, rows, :].astype(F32))
+            block(FIRST[level] + i * 16, None)
             return carry
 
         def paired(i, carry, level=level, singles=singles):
             other = pl.ds(pl.multiple_of(level * 64 + i * 16, 16), 16)
-            block(
-                FIRST[level] + singles + i * 16,
-                lambda c, rows: 0.5 * (vis_ref[c, rows, :].astype(F32) + pair_ref[c, other, :].astype(F32)),
-            )
+            block(FIRST[level] + singles + i * 16, other)
             return carry
 
         lax.fori_loop(0, singles // 16, single, 0, unroll=2)
@@ -307,21 +367,26 @@
         for c in range(0, 8, 2):
             cols = slice(c * 128, (c + 2) * 128)
             cal[rows, cols] = dot(cal[rows, cols], mean).astype(BF16)
-    for c in range(0, 8, 2):
-        part = dot(weight_ref[...], cal[:, c * 128 : (c + 2) * 128])
+    low = low_lanes(256)
+    for g in range(4):
+        block_cols = cal[:, g * 256 : (g + 1) * 256]
+        even = dot(weight_ref[0], block_cols)
+        odd = dot(weight_ref[1], block_cols)
+        part = jnp.where(
+            low, even[:, lanes(0)] + roll64(odd[:, lanes(0)]), roll64(even[:, lanes(1)]) + odd[:, lanes(1)]
+        ).astype(BF16)
         for m in range(32):
-            for half in range(2):
-                row = ROWS + (c + half) * 8
-                out_ref[m, row : row + 8, :] = part[m * 8 : (m + 1) * 8, lanes(half)].astype(BF16)
-
-
-def calibrate(gains, left, right, weight, vis, pair):
+            row = ROWS + g * 8
+            out_ref[m, row : row + 8, :] = part[m * 8 : (m + 1) * 8, :]
+
+
+def calibrate(me, gains, left, right, weight, vis, x, z, xz):
     vmem = pl.BlockSpec(memory_space=pltpu.VMEM)
     return pl.pallas_call(
         calibrate_kernel,
-        in_specs=[vmem] * 6,
+        in_specs=[pl.BlockSpec(memory_space=pltpu.SMEM)] + [vmem] * 8,
         out_specs=vmem,
-        out_shape=jax.ShapeDtypeStruct((32, ROWS + 64, 128), BF16),
+        out_shape=jax.ShapeDtypeStruct((32, ROWS + 32, 128), BF16),
         scratch_shapes=[
             pltpu.VMEM((256, 1024), F32),
             pltpu.VMEM((KEEP, 1024), F32),
@@ -331,7 +396,7 @@
         ],
         compiler_params=pltpu.CompilerParams(vmem_limit_bytes=VMEM_LIMIT),
         name="calibrate",
-    )(gains, left, right, weight, vis, pair)
+    )(me, gains, left, right, weight, vis, x, z, xz)
 
 
 def finish_kernel(recv_ref, pick_ref, lane_ref, time_ref, avg_ref, grid_ref, means):
@@ -353,25 +418,37 @@
                     means[x + 2 * j + 1, row : row + 8, :] = value
 
     pick = pick_ref[:, 0:MEANS]
-    lane = lane_ref[...]
+    index = [lane_ref[0], lane_ref[1]]
+    low = low_lanes(128)
 
     def step(i, carry):
-        both = jnp.concatenate([means[2 * i], means[2 * i + 1]], axis=1).astype(BF16)
+        first = (i >> 3) * 16 + (i & 7)
+        both = jnp.concatenate([means[first], means[first + 8]], axis=1).astype(BF16)
         rows = dot(pick, both)
+        for bit in range(2):
+            half = [
+                jnp.take_along_axis(rows[:, lanes(k)], index[bit], axis=1, mode="promise_in_bounds") for k in range(2)
+            ]
+            avg_ref[first + 8 * bit] = jnp.where(low, half[0], half[1]).astype(BF16).reshape(8, 16, 128)
+        return carry
+
+    lax.fori_loop(0, 16, step, 0, unroll=8)
+
+    low8 = low_lanes(8)
+    for g in range(4):
+        row = ROWS + g * 8
+        total = []
         for half in range(2):
-            value = jnp.take_along_axis(rows[:, lanes(half)], lane, axis=1, mode="promise_in_bounds")
-            avg_ref[2 * i + half] = value.astype(BF16).reshape(8, 16, 128)
-        return carry
-
-    lax.fori_loop(0, 16, step, 0, unroll=8)
-
-    for c in range(8):
-        row = ROWS + c * 8
-        total = recv_ref[0, row : row + 8, :].astype(F32)
-        for t in range(1, 32):
-            total = total + recv_ref[t, row : row + 8, :].astype(F32)
+            sources = [x * 8 + z for x in (half, half + 2) for z in range(8)]
+            value = recv_ref[sources[0], row : row + 8, :].astype(F32)
+            for source in sources[1:]:
+                value = value + recv_ref[source, row : row + 8, :].astype(F32)
+            total.append(value)
+        even = jnp.where(low8, total[0], roll64(total[1]))
+        odd = jnp.where(low8, roll64(total[0]), total[1])
         for u in range(8):
-            grid_ref[u, c : c + 1, :] = total[u : u + 1, :]
+            grid_ref[u, 2 * g : 2 * g + 1, :] = even[u : u + 1, :]
+            grid_ref[u, 2 * g + 1 : 2 * g + 2, :] = odd[u : u + 1, :]
 
 
 def finish(recv, pick, lane, time):
@@ -393,11 +470,13 @@
 def shards(visibilities, station_gains, station_pairs, average_bands, tile_map, baseline_order):
     me = lax.axis_index("tm").reshape(1)
     bands = average_bands.T
-    keep, send, hot, position = route(me, bands, baseline_order[None, :], visibilities[0])
-    pair = lax.ppermute(send, "tm", [(m, m ^ 1) for m in range(32)])
-    gains = lax.all_to_all(cut_gains(station_gains, position), "chan", 0, 0, tiled=True)
+    keep, x, z, xz, hot, position = route(me, bands, baseline_order[None, :], visibilities[0])
+    x, z, xz = [
+        lax.ppermute(value, "tm", [(m, m ^ bits) for m in range(32)]) for value, bits in ((x, 8), (z, 1), (xz, 9))
+    ]
+    gains = lax.all_to_all(cut_gains(me, station_gains, position), "chan", 0, 0, tiled=True)
     left, right, weight, pick, lane, time = tables(me, station_pairs.T, bands, tile_map.T, hot, position)
-    payload = calibrate(gains, left, right, weight, keep, pair)
+    payload = calibrate(me, gains, left, right, weight, keep, x, z, xz)
     recv = lax.all_to_all(payload, "tm", 0, 0, tiled=True)
     averaged, gridded = finish(recv, pick, lane, time)
     return averaged, gridded

time: 60.9 us -> 58.2 us (0.956)
  blocking collectives: 36.9 us -> 31 us
  Pallas kernels: 7.39 us -> 10.1 us
  starting transfers between devices: 5.51 us -> 8.08 us
  waiting for transfers between devices: 7.43 us -> 5.36 us
    all_to_all x1, blocking collectives: 36.9 us -> 31 us  [shards(): recv = lax.all_to_all(payload, 'tm', 0, 0, tiled=True)]
    all_to_all x1, waiting for transfers between devices: 7.43 us -> 5.35 us  [shards(): lax.all_to_all(cut_gains(me, station_gains, position), 'chan', 0, 0, tile...]
    ppermute x1 -> x3, starting transfers between devices: 1.93 us -> 3.49 us  [shards(): lax.ppermute(value, 'tm', [(m, m ^ bits) for m in range(32)])]
    pallas_call x2, Pallas kernels: 3.11 us -> 4.31 us  [the longest x1 3.45 us: calibrate(): pl.pallas_call(calibrate_kernel, in_specs=[pl.BlockSpec(memory_space=pltp...]
    all_to_all x1, starting transfers between devices: 3.58 us -> 4.6 us  [shards(): lax.all_to_all(cut_gains(me, station_gains, position), 'chan', 0, 0, tile...]
    pallas_call x1, Pallas kernels: 1.38 us -> 2.13 us  [route(): pl.pallas_call(route_kernel, in_specs=[pl.BlockSpec(memory_space=pltpu.SM...]
    pallas_call x1, Pallas kernels: 2.17 us -> 2.87 us  [finish(): pl.pallas_call(finish_kernel, in_specs=[vmem] * 4, out_specs=[vmem] * 2,...]
  transfers between devices with their start and end apart: 2 -> 4, of which waited for: 1 -> 1; matrix products, arithmetic and copies ran while one was open for 0% -> 0% of each run, Pallas kernels for 3% -> 3%
where the time goes in v4:
time: 58.2 us; the launch traced here: 57.8 us
  blocking collectives  31 us (53%)
  Pallas kernels  10.1 us (17%)
  starting transfers between devices  8.08 us (14%)
  waiting for transfers between devices  5.36 us (9%)
  local copies, waits for them, and re-layouts  2.59 us (4%)
  between operations  0.69 us (1%)
    all_to_all x1, blocking collectives, shards(): recv = lax.all_to_all(payload, 'tm', 0, 0, tiled=True)  31 us
    all_to_all x1, waiting for transfers between devices, shards(): lax.all_to_all(cut_gains(me, station_gains, position), 'chan', 0, 0, tile...  5.35 us
    all_to_all x1, starting transfers between devices, shards(): lax.all_to_all(cut_gains(me, station_gains, position), 'chan', 0, 0, tile...  4.6 us
    ppermute x3, starting transfers between devices, shards(): lax.ppermute(value, 'tm', [(m, m ^ bits) for m in range(32)])  3.49 us
    pallas_call x1, Pallas kernels, calibrate(): pl.pallas_call(calibrate_kernel, in_specs=[pl.BlockSpec(memory_space=pltp...  3.45 us
    pallas_call x1, Pallas kernels, finish(): pl.pallas_call(finish_kernel, in_specs=[vmem] * 4, out_specs=[vmem] * 2,...  2.87 us
    unnamed x12, local copies, waits for them, and re-layouts  2.59 us
    pallas_call x1, Pallas kernels, route(): pl.pallas_call(route_kernel, in_specs=[pl.BlockSpec(memory_space=pltpu.SM...  2.13 us
  transfers between devices with their start and end apart: 4, of which 1 were waited for; matrix products, arithmetic and copies ran while one was open for 0% of the time, Pallas kernels for 3%

profile of v4, /device:TPU:32, one launch (start us, length us, event | category | flops | bytes accessed | tf_op | source)
XLA Modules:
  0.0 57.8 jit_solution(2605338082523849360)
XLA Ops:
  0.6 0.0 copy-start.2
  0.6 0.0 copy-start.3
  0.7 0.7 %copy-done.2 = s32[512,2]{0,1:T(2,128)S(1)} copy-done((s32[512,2]{0,1:T(2,128)S(1)}, s32[512,2]{0,1:T(2,128)}, u32[]{:S(2)}) %copy-start.2) | copy-done | bytes 4120
  1.3 0.0 copy-done.3
  1.3 0.0 copy-start
  1.3 1.2 %copy-done = bf16[1,8,512,128]{3,2,1,0:T(8,128)(2,1)S(1)} copy-done((bf16[1,8,512,128]{3,2,1,0:T(8,128)(2,1)S(1)}, bf16[1,8,512,128]{3,2,1,0:T(8,128)(2,1)}, u32[]{:S(2)}) %copy-start) | copy-done | bytes 1048600
  2.6 0.0 copy-start.1
  2.6 2.1 %route.1 = (bf16[8,320,128]{2,1,0:T(8,128)(2,1)S(1)}, bf16[4,320,128]{2,1,0:T(8,128)(2,1)S(1)}, bf16[4,192,128]{2,1,0:T(8,128)(2,1)}, bf16[4,192,128]{2,1,0:T(8,...) custom-call(s32[1]{0:T(128)} %bitcast.me_ref, s32[2,512]{1,0:T(2,128)S(1)} %bitcast.7, ...), custom_call_target="tpu_custom_call" | custom-call | tf_op jit(solution)/shard_map/route/pallas_call | solution.py:133
  4.7 1.5 %collective-permute-start = (bf16[4,320,128]{2,1,0:T(8,128)(2,1)S(1)}, bf16[4,320,128]{2,1,0:T(8,128)(2,1)S(1)}, u32[]{:S(2)}, u32[]{:S(2)}) collective-permute-start(bf16[4,320,128]{2,1,0:T(8,128)(2,1)S(1)} %get-tuple-element.20), channel_id=1, source_target_pairs={{0,64},{8,72},{16,80},{24,88},{32,96},{40,104},{48,112},{56,120},{... | collective-permute-start | bytes 983048 | tf_op jit(solution)/shard_map/ppermute | solution.py:475
  6.2 0.3 collective-permute-start.1
  6.5 1.6 %collective-permute-start.2 = (bf16[4,192,128]{2,1,0:T(8,128)(2,1)S(1)}, bf16[4,192,128]{2,1,0:T(8,128)(2,1)S(1)}, u32[]{:S(2)}, u32[]{:S(2)}) collective-permute-start(bf16[4,192,128]{2,1,0:T(8,128)(2,1)S(1)} %get-tuple-element.22), channel_id=1, source_target_pairs={{0,72},{8,64},{16,88},{24,80},{32,104},{40,96},{48,120},{56,112},{... | collective-permute-start | bytes 589832 | tf_op jit(solution)/shard_map/ppermute | solution.py:475
  8.2 0.0 copy-done.1
  8.2 0.9 %cut_gains.1 = bf16[8,96,128]{2,1,0:T(8,128)(2,1)} custom-call(s32[1]{0:T(128)} %bitcast.me_ref, f32[8,24,1024]{2,1,0:T(8,128)S(1)} %copy-done.1, f32[8,512]{1,0:T(8,128)S(1)} %get-tuple-element.14.after_ref.position_ref), custom_call_target="tpu_custom_call" | custom-call | tf_op jit(solution)/shard_map/cut_gains/pallas_call | solution.py:69
  9.0 0.0 copy-start.4
  9.0 4.6 %all-to-all-start = ((bf16[8,96,128]{2,1,0:T(8,128)(2,1)}), bf16[8,96,128]{2,1,0:T(8,128)(2,1)S(1)}, u32[]{:S(2)}, u32[]{:S(2)}) async-start(bf16[8,96,128]{2,1,0:T(8,128)(2,1)} %cut_gains.1), calls=%async_computation | async-start | bytes 393216 | tf_op jit(solution)/shard_map/all_to_all | solution.py:477
  13.6 0.0 copy-start.5
  13.6 0.0 copy-done.4
  13.6 0.7 %copy-done.5 = s32[512,2]{0,1:T(2,128)S(1)} copy-done((s32[512,2]{0,1:T(2,128)S(1)}, s32[512,2]{0,1:T(2,128)}, u32[]{:S(2)}) %copy-start.5) | copy-done | bytes 4120
  14.3 0.8 %tables.1 = (bf16[320,256]{1,0:T(8,128)(2,1)S(1)}, bf16[320,256]{1,0:T(8,128)(2,1)S(1)}, bf16[2,256,320]{2,1,0:T(8,128)(2,1)S(1)}, bf16[128,128]{1,0:T(8,128)(2,...) custom-call(s32[1]{0:T(128)} %bitcast.me_ref, s32[2,512]{1,0:T(2,128)S(1)} %bitcast.11, s32[2,512]{1,0:T(2,128)S(1)} %bitcast.8, ...), custom_call_target="tpu_custom_call" | custom-call | flops 1000000000 | bytes 4000000 | tf_op jit(solution)/shard_map/tables/pallas_call | solution.py:222
  15.1 5.4 %all-to-all-done.gain_ref = bf16[8,96,128]{2,1,0:T(8,128)(2,1)S(1)} async-done(((bf16[8,96,128]{2,1,0:T(8,128)(2,1)}), bf16[8,96,128]{2,1,0:T(8,128)(2,1)S(1)}, u32[]{:S(2)}, u32[]{:S(2)}) %all-to-all-start) | async-done | bytes 196640 | tf_op jit(solution)/shard_map/all_to_all | solution.py:477
  20.5 0.0 collective-permute-done.1.z_ref
  20.5 0.0 collective-permute-done.2.xz_ref
  20.5 0.0 collective-permute-done.x_ref
  20.5 3.5 %calibrate.1 = bf16[32,80,128]{2,1,0:T(8,128)(2,1)S(1)} custom-call(s32[1]{0:T(128)} %bitcast.me_ref, bf16[8,96,128]{2,1,0:T(8,128)(2,1)S(1)} %all-to-all-done.gain_ref, bf16[320,256]{1,0:T(8,128)(2,1)S(1)} %get-tuple-element.16.left_ref, bf16[320,256]{1,0:T(8,128)(2,1)S(1)} %get-tuple-element.17.right_ref, ...), custom_call_target="tpu_custom_call" | custom-call | tf_op jit(solution)/shard_map/calibrate/pallas_call | solution.py:385
  23.9 31.0 %all_to_all.10.recv_ref = bf16[32,80,128]{2,1,0:T(8,128)(2,1)S(1)} all-to-all(bf16[32,80,128]{2,1,0:T(8,128)(2,1)S(1)} %calibrate.1), channel_id=1, replica_groups=mesh['tm'=32,'chan'=8] {'tm'}, dimensions={0} | all-to-all | bytes 1310720 | tf_op jit(solution)/shard_map/all_to_all | solution.py:480
  55.0 2.9 %finish.1 = (bf16[32,8,16,128]{3,2,1,0:T(8,128)(2,1)}, f32[8,8,128]{2,1,0:T(8,128)}) custom-call(bf16[32,80,128]{2,1,0:T(8,128)(2,1)S(1)} %all_to_all.10.recv_ref, bf16[128,128]{1,0:T(8,128)(2,1)S(1)} %get-tuple-element.23.pick_ref, s32[2,128,128]{2,1,0:T(8,128)S(1)} %get-tuple-element.24.lane_ref, f32[128,128]{1,0:T(8,128)S(1)} %get-tuple-element.25.time_ref), custom_call_target="tpu_custom_call" | custom-call | tf_op jit(solution)/shard_map/finish/pallas_call | solution.py:456
Async XLA Ops:
  0.6 0.7 %copy-start.2 = (s32[512,2]{0,1:T(2,128)S(1)}, s32[512,2]{0,1:T(2,128)}, u32[]{:S(2)}) copy-start(s32[512,2]{0,1:T(2,128)} %param.9) | copy-start | bytes 12292
  0.6 0.7 %copy-start.3 = (s32[512]{0:T(512)S(1)}, s32[512]{0:T(512)}, u32[]{:S(2)}) copy-start(s32[512]{0:T(512)} %param.11) | copy-start | bytes 6148
  1.3 1.2 %copy-start = (bf16[1,8,512,128]{3,2,1,0:T(8,128)(2,1)S(1)}, bf16[1,8,512,128]{3,2,1,0:T(8,128)(2,1)}, u32[]{:S(2)}) copy-start(bf16[1,8,512,128]{3,2,1,0:T(8,128)(2,1)} %param.6) | copy-start | bytes 3145732
  2.6 5.6 %copy-start.1 = (f32[8,24,1024]{2,1,0:T(8,128)S(1)}, f32[8,24,1024]{2,1,0:T(8,128)}, u32[]{:S(2)}) copy-start(f32[8,24,1024]{2,1,0:T(8,128)} %gain_ref.1) | copy-start | bytes 2359300
  4.7 15.8 %collective-permute-start = (bf16[4,320,128]{2,1,0:T(8,128)(2,1)S(1)}, bf16[4,320,128]{2,1,0:T(8,128)(2,1)S(1)}, u32[]{:S(2)}, u32[]{:S(2)}) collective-permute-start(bf16[4,320,128]{2,1,0:T(8,128)(2,1)S(1)} %get-tuple-element.20), channel_id=1, source_target_pairs={{0,64},{8,72},{16,80},{24,88},{32,96},{40,104},{48,112},{56,120},{... | collective-permute-start | bytes 983048 | tf_op jit(solution)/shard_map/ppermute | solution.py:475
  6.2 14.3 %collective-permute-start.1 = (bf16[4,192,128]{2,1,0:T(8,128)(2,1)}, bf16[4,192,128]{2,1,0:T(8,128)(2,1)S(1)}, u32[]{:S(2)}, u32[]{:S(2)}) collective-permute-start(bf16[4,192,128]{2,1,0:T(8,128)(2,1)} %get-tuple-element.21), channel_id=1, source_target_pairs={{0,8},{8,0},{16,24},{24,16},{32,40},{40,32},{48,56},{56,48},{64,72... | collective-permute-start | bytes 589832 | tf_op jit(solution)/shard_map/ppermute | solution.py:475
  6.5 13.9 %collective-permute-start.2 = (bf16[4,192,128]{2,1,0:T(8,128)(2,1)S(1)}, bf16[4,192,128]{2,1,0:T(8,128)(2,1)S(1)}, u32[]{:S(2)}, u32[]{:S(2)}) collective-permute-start(bf16[4,192,128]{2,1,0:T(8,128)(2,1)S(1)} %get-tuple-element.22), channel_id=1, source_target_pairs={{0,72},{8,64},{16,88},{24,80},{32,104},{40,96},{48,120},{56,112},{... | collective-permute-start | bytes 589832 | tf_op jit(solution)/shard_map/ppermute | solution.py:475
  9.0 4.6 %copy-start.4 = (s32[512,32]{0,1:T(8,128)S(1)}, s32[512,32]{0,1:T(8,128)}, u32[]{:S(2)}) copy-start(s32[512,32]{0,1:T(8,128)} %param.10) | copy-start | bytes 196612
  9.0 11.4 %all-to-all-start = ((bf16[8,96,128]{2,1,0:T(8,128)(2,1)}), bf16[8,96,128]{2,1,0:T(8,128)(2,1)S(1)}, u32[]{:S(2)}, u32[]{:S(2)}) async-start(bf16[8,96,128]{2,1,0:T(8,128)(2,1)} %cut_gains.1), calls=%async_computation | async-start | bytes 393216 | tf_op jit(solution)/shard_map/all_to_all | solution.py:477
  13.6 0.7 %copy-start.5 = (s32[512,2]{0,1:T(2,128)S(1)}, s32[512,2]{0,1:T(2,128)}, u32[]{:S(2)}) copy-start(s32[512,2]{0,1:T(2,128)} %param.8) | copy-start | bytes 12292

commit v5 on v4

--- a/solution.py
+++ b/solution.py
@@ -8,6 +8,7 @@
 
 KEEP = 320
 SEND = 192
+STACK = 384
 FIRST = (0, 96, 192)
 SIZES = (96, 96, 128)
 UNIT_ROW = (0, 16, 24, 8, 32, 36, 12, 14, 40, 42)
@@ -79,7 +80,7 @@
     )(me, gains, after)
 
 
-def route_kernel(me_ref, bands_ref, order_ref, vis_ref, keep_out, x_out, z_out, xz_out, hot_out, position_out):
+def slots_kernel(me_ref, bands_ref, order_ref, hot_out, position_out):
     me = me_ref[0]
     nb = order_ref.shape[1]
     info = rows_of([bands_ref[0:1, :].astype(F32), bands_ref[1:2, :].astype(F32)], nb).astype(BF16)
@@ -104,9 +105,30 @@
     single = jnp.where(chan_here == 0, 0, jnp.where(chan_here == 1, 3, 6)) + place
     unit = jnp.where(kind < 3, single, jnp.where(side == (me & 1), kept, sent))
     slot = unit * 32 + (iota((1, nb), 1) >> 4)
-    slot_hot = dot_t(one_hot(iota((nb, nb), 0) == slot), order_hot).astype(BF16)
-    first_half = ((me >> 3) & 1) == 0
-    low = low_lanes(nb)
+    hot_out[...] = dot_t(one_hot(iota((nb, nb), 0) == slot), order_hot).astype(BF16)
+    position_out[...] = rows_of(
+        [time_here, chan_here.astype(F32), kind.astype(F32), side.astype(F32), place.astype(F32)], nb
+    )
+
+
+def slots(me, bands, order):
+    nb = order.shape[1]
+    vmem = pl.BlockSpec(memory_space=pltpu.VMEM)
+    return pl.pallas_call(
+        slots_kernel,
+        in_specs=[pl.BlockSpec(memory_space=pltpu.SMEM), vmem, vmem],
+        out_shape=[jax.ShapeDtypeStruct((nb, nb), BF16), jax.ShapeDtypeStruct((8, nb), F32)],
+        compiler_params=pltpu.CompilerParams(vmem_limit_bytes=VMEM_LIMIT),
+        cost_estimate=pl.CostEstimate(flops=1_000_000_000, bytes_accessed=3_000_000, transcendentals=0),
+        name="slots",
+    )(me, bands, order)
+
+
+def route_kernel(me_ref, hot_ref, vis_ref, keep_out, x_out, z_out, xz_out):
+    me = me_ref[0]
+    slot_hot = hot_ref[...]
+    nb = slot_hot.shape[0]
+    mine = low_lanes(nb) == (((me >> 3) & 1) == 0)
     for g in range(4):
         both = jnp.concatenate([vis_ref[2 * g], vis_ref[2 * g + 1]], axis=1)
         moved = dot(slot_hot, both)
@@ -114,36 +136,26 @@
         b = moved[:, lanes(1)]
         keep_out[2 * g] = a[:KEEP].astype(BF16)
         keep_out[2 * g + 1] = b[:KEEP].astype(BF16)
-        lower = jnp.where(low, a, roll64(b))
-        upper = jnp.where(low, roll64(a), b)
-        here = jnp.where(first_half, lower, upper).astype(BF16)
-        there = jnp.where(first_half, upper, lower).astype(BF16)
+        there = jnp.where(mine, roll64(a), b).astype(BF16)
         x_out[g] = there[:KEEP]
         xz_out[g] = there[KEEP:]
-        z_out[g] = here[KEEP:]
-    hot_out[...] = slot_hot[:KEEP]
-    position_out[...] = rows_of(
-        [time_here, chan_here.astype(F32), kind.astype(F32), side.astype(F32), place.astype(F32)], nb
-    )
-
-
-def route(me, bands, order, vis):
-    nb = order.shape[1]
+        z_out[g] = jnp.where(mine[KEEP:], a[KEEP:], roll64(b[KEEP:])).astype(BF16)
+
+
+def route(me, hot, vis):
     vmem = pl.BlockSpec(memory_space=pltpu.VMEM)
     return pl.pallas_call(
         route_kernel,
-        in_specs=[pl.BlockSpec(memory_space=pltpu.SMEM)] + [vmem] * 3,
+        in_specs=[pl.BlockSpec(memory_space=pltpu.SMEM), vmem, vmem],
         out_shape=[
             jax.ShapeDtypeStruct((8, KEEP, 128), BF16),
             jax.ShapeDtypeStruct((4, KEEP, 128), BF16),
             jax.ShapeDtypeStruct((4, SEND, 128), BF16),
             jax.ShapeDtypeStruct((4, SEND, 128), BF16),
-            jax.ShapeDtypeStruct((KEEP, nb), BF16),
-            jax.ShapeDtypeStruct((8, nb), F32),
         ],
         compiler_params=pltpu.CompilerParams(vmem_limit_bytes=VMEM_LIMIT),
         name="route",
-    )(me, bands, order, vis)
+    )(me, hot, vis)
 
 
 def tables_kernel(
@@ -161,16 +173,17 @@
             tile = jnp.where(time_level == level, tiles_ref[pl.ds(start, 1), :], tile)
         tiles.append(tile.astype(F32))
     info = rows_of([time_level.astype(F32)] + tiles, nb).astype(BF16)
-    slot_hot = hot_ref[...]
+    slot_hot = hot_ref[0:KEEP, :]
     left_out[...] = dot_t(slot_hot, one_hot(iota((256, nb), 0) == pairs_ref[0:1, :])).astype(BF16)
     right_out[...] = dot_t(slot_hot, one_hot(iota((256, nb), 0) == pairs_ref[1:2, :])).astype(BF16)
 
     at_slot = dot_t(info, slot_hot)
     time_slot = at_slot[0:1, :]
     weight = jnp.where(time_slot <= 1.0, 1.0, jnp.where(time_slot == 2.0, 0.5, 0.25))
+    weight_out[...] = jnp.zeros((256, 2 * STACK), BF16)
     for i in range(2):
         tile_slot = at_slot[1 + i : 2 + i, :].astype(jnp.int32)
-        weight_out[i] = jnp.where(iota((256, KEEP), 0) == tile_slot, weight, 0.0).astype(BF16)
+        weight_out[:, i * STACK : i * STACK + KEEP] = jnp.where(iota((256, KEEP), 0) == tile_slot, weight, 0.0).astype(BF16)
 
     own = dot(
         position_ref[...].astype(BF16), one_hot(iota((nb, 128), 0) == me * 16 + (iota((nb, 128), 1) & 15))
@@ -225,7 +238,7 @@
         out_shape=[
             jax.ShapeDtypeStruct((KEEP, 256), BF16),
             jax.ShapeDtypeStruct((KEEP, 256), BF16),
-            jax.ShapeDtypeStruct((2, 256, KEEP), BF16),
+            jax.ShapeDtypeStruct((256, 2 * STACK), BF16),
             jax.ShapeDtypeStruct((128, 128), BF16),
             jax.ShapeDtypeStruct((2, 128, 128), jnp.int32),
             jax.ShapeDtypeStruct((128, 128), F32),
@@ -284,7 +297,7 @@
 
 
 def calibrate_kernel(
-    me_ref, gain_ref, left_ref, right_ref, weight_ref, vis_ref, x_ref, z_ref, xz_ref, out_ref, gains, gl, gr, cal, wide
+    me_ref, gain_ref, left_ref, right_ref, weight_ref, vis_ref, x_ref, z_ref, xz_ref, out_ref, gains, gl, gr, cal, wide, stack
 ):
     stations = gain_ref.shape[1] // 4
     low = low_lanes(stations)
@@ -299,23 +312,29 @@
     gl[...] = dot(left_ref[...], table)
     gr[...] = dot(right_ref[...], table)
 
-    first_half = ((me_ref[0] >> 3) & 1) == 0
-    mine = low_lanes(16) == first_half
-
-    def spread(ref, g, rows, front):
+    mine = low_lanes(16) == (((me_ref[0] >> 3) & 1) == 0)
+
+    def spread(ref, g, rows):
         both = ref[g, rows, :].astype(F32)
-        swapped = roll64(both)
-        return jnp.where(front, both, swapped), jnp.where(front, swapped, both)
-
-    def block(first, other):
+        return both, roll64(both)
+
+    def stack_rows(g, start, rows, a, b):
+        low = low_lanes(a.shape[0])
+        stack[pl.ds(start, rows), lanes(g)] = jnp.where(low, a, roll64(b)).astype(BF16)
+        stack[pl.ds(STACK + start, rows), lanes(g)] = jnp.where(low, roll64(a), b).astype(BF16)
+
+    for part in (KEEP, STACK + KEEP):
+        stack[part : part + STACK - KEEP, :] = jnp.zeros((STACK - KEEP, 512), BF16)
+
+    def block(first, other, level):
         rows = pl.ds(pl.multiple_of(first, 16), 16)
         value = []
         for g in range(4):
-            theirs = spread(x_ref, g, rows, jnp.logical_not(first_half))
+            theirs = spread(x_ref, g, rows)
             pair = [jnp.where(mine, vis_ref[2 * g + i, rows, :].astype(F32), theirs[i]) for i in range(2)]
             if other is not None:
-                near = spread(z_ref, g, other, first_half)
-                far = spread(xz_ref, g, other, jnp.logical_not(first_half))
+                near = spread(z_ref, g, other)
+                far = spread(xz_ref, g, other)
                 pair = [0.5 * (pair[i] + jnp.where(mine, near[i], far[i])) for i in range(2)]
             value.extend(pair)
         result = jones_apply(
@@ -323,20 +342,23 @@
         )
         for c in range(8):
             cal[rows, lanes(c)] = result[c].astype(BF16)
+        if level == 0:
+            for g in range(4):
+                stack_rows(g, pl.multiple_of(first, 16), 16, result[2 * g], result[2 * g + 1])
 
     for level, singles in ((0, 32), (1, 32), (2, 64)):
 
         def single(i, carry, level=level):
-            block(FIRST[level] + i * 16, None)
+            block(FIRST[level] + i * 16, None, level)
             return carry
 
         def paired(i, carry, level=level, singles=singles):
             other = pl.ds(pl.multiple_of(level * 64 + i * 16, 16), 16)
-            block(FIRST[level] + singles + i * 16, other)
+            block(FIRST[level] + singles + i * 16, other, level)
             return carry
 
         lax.fori_loop(0, singles // 16, single, 0, unroll=2)
-        lax.fori_loop(0, 4, paired, 0, unroll=2)
+        lax.fori_loop(0, 4, paired, 0, unroll=4)
 
     for u in range(3):
         for c in range(8):
@@ -364,20 +386,15 @@
         group = iota((256, 256), 0) >> level == iota((256, 256), 1) >> level
         mean = jnp.where(group, 0.5**level, 0.0).astype(BF16)
         rows = slice(FIRST[level], FIRST[level] + SIZES[level])
-        for c in range(0, 8, 2):
-            cols = slice(c * 128, (c + 2) * 128)
-            cal[rows, cols] = dot(cal[rows, cols], mean).astype(BF16)
-    low = low_lanes(256)
-    for g in range(4):
-        block_cols = cal[:, g * 256 : (g + 1) * 256]
-        even = dot(weight_ref[0], block_cols)
-        odd = dot(weight_ref[1], block_cols)
-        part = jnp.where(
-            low, even[:, lanes(0)] + roll64(odd[:, lanes(0)]), roll64(even[:, lanes(1)]) + odd[:, lanes(1)]
-        ).astype(BF16)
+        for g in range(4):
+            value = dot(cal[rows, g * 256 : (g + 1) * 256], mean)
+            stack_rows(g, FIRST[level], SIZES[level], value[:, lanes(0)], value[:, lanes(1)])
+    for g in range(0, 4, 2):
+        part = dot(weight_ref[...], stack[:, g * 128 : (g + 2) * 128]).astype(BF16)
         for m in range(32):
-            row = ROWS + g * 8
-            out_ref[m, row : row + 8, :] = part[m * 8 : (m + 1) * 8, :]
+            for i in range(2):
+                row = ROWS + (g + i) * 8
+                out_ref[m, row : row + 8, :] = part[m * 8 : (m + 1) * 8, lanes(i)]
 
 
 def calibrate(me, gains, left, right, weight, vis, x, z, xz):
@@ -393,6 +410,7 @@
             pltpu.VMEM((KEEP, 1024), F32),
             pltpu.VMEM((KEEP, 1024), BF16),
             pltpu.VMEM((32 * ROWS, 128), F32),
+            pltpu.VMEM((2 * STACK, 512), BF16),
         ],
         compiler_params=pltpu.CompilerParams(vmem_limit_bytes=VMEM_LIMIT),
         name="calibrate",
@@ -470,11 +488,12 @@
 def shards(visibilities, station_gains, station_pairs, average_bands, tile_map, baseline_order):
     me = lax.axis_index("tm").reshape(1)
     bands = average_bands.T
-    keep, x, z, xz, hot, position = route(me, bands, baseline_order[None, :], visibilities[0])
+    hot, position = slots(me, bands, baseline_order[None, :])
+    keep, x, z, xz = route(me, hot, visibilities[0])
     x, z, xz = [
         lax.ppermute(value, "tm", [(m, m ^ bits) for m in range(32)]) for value, bits in ((x, 8), (z, 1), (xz, 9))
     ]
-    gains = lax.all_to_all(cut_gains(me, station_gains, position), "chan", 0, 0, tiled=True)
+    gains = lax.all_to_all(cut_gains(me, station_gains, keep), "chan", 0, 0, tiled=True)
     left, right, weight, pick, lane, time = tables(me, station_pairs.T, bands, tile_map.T, hot, position)
     payload = calibrate(me, gains, left, right, weight, keep, x, z, xz)
     recv = lax.all_to_all(payload, "tm", 0, 0, tiled=True)

time: 58.2 us -> 56.5 us (0.971)
  local copies, waits for them, and re-layouts: 2.59 us -> 1.76 us
  Pallas kernels: 10.1 us -> 9.29 us
    pallas_call x1, Pallas kernels: 3.45 us -> 2.42 us  [calibrate(): pl.pallas_call(calibrate_kernel, in_specs=[pl.BlockSpec(memory_space=pltp...]
    unnamed x12, local copies, waits for them, and re-layouts: 2.59 us -> 1.76 us
    pallas_call x0 -> x1, Pallas kernels: none -> 0.82 us  [slots(): pl.pallas_call(slots_kernel, in_specs=[pl.BlockSpec(memory_space=pltpu.SM...]
    pallas_call x1, Pallas kernels: 2.13 us -> 1.54 us  [route(): pl.pallas_call(route_kernel, in_specs=[pl.BlockSpec(memory_space=pltpu.SM...]
where the time goes in v5:
time: 56.5 us; the launch traced here: 56.2 us
  blocking collectives  31 us (55%)
  Pallas kernels  9.29 us (16%)
  starting transfers between devices  8.09 us (14%)
  waiting for transfers between devices  5.36 us (9%)
  local copies, waits for them, and re-layouts  1.76 us (3%)
  between operations  0.69 us (1%)
    all_to_all x1, blocking collectives, shards(): recv = lax.all_to_all(payload, 'tm', 0, 0, tiled=True)  31 us
    all_to_all x1, waiting for transfers between devices, shards(): lax.all_to_all(cut_gains(me, station_gains, keep), 'chan', 0, 0, tiled=True)  5.35 us
    all_to_all x1, starting transfers between devices, shards(): lax.all_to_all(cut_gains(me, station_gains, keep), 'chan', 0, 0, tiled=True)  4.6 us
    ppermute x3, starting transfers between devices, shards(): lax.ppermute(value, 'tm', [(m, m ^ bits) for m in range(32)])  3.49 us
    pallas_call x1, Pallas kernels, finish(): pl.pallas_call(finish_kernel, in_specs=[vmem] * 4, out_specs=[vmem] * 2,...  2.87 us
    pallas_call x1, Pallas kernels, calibrate(): pl.pallas_call(calibrate_kernel, in_specs=[pl.BlockSpec(memory_space=pltp...  2.42 us
    unnamed x12, local copies, waits for them, and re-layouts  1.76 us
    pallas_call x1, Pallas kernels, route(): pl.pallas_call(route_kernel, in_specs=[pl.BlockSpec(memory_space=pltpu.SM...  1.54 us
  transfers between devices with their start and end apart: 4, of which 1 were waited for; matrix products, arithmetic and copies ran while one was open for 0% of the time, Pallas kernels for 3%

profile of v5, /device:TPU:32, one launch (start us, length us, event | category | flops | bytes accessed | tf_op | source)
XLA Modules:
  0.0 56.2 jit_solution(3192270687438096995)
XLA Ops:
  0.6 0.0 copy-start.3
  0.6 0.0 copy-start.5
  0.7 0.7 %copy-done.3 = s32[512,2]{0,1:T(2,128)S(1)} copy-done((s32[512,2]{0,1:T(2,128)S(1)}, s32[512,2]{0,1:T(2,128)}, u32[]{:S(2)}) %copy-start.3) | copy-done | bytes 4120
  1.3 0.0 copy-done.5
  1.3 0.0 copy-start
  1.3 0.8 %slots.1 = (bf16[512,512]{1,0:T(8,128)(2,1)S(1)}, f32[8,512]{1,0:T(8,128)S(1)}) custom-call(s32[1]{0:T(128)} %bitcast.me_ref, s32[2,512]{1,0:T(2,128)S(1)} %bitcast.8, s32[1,512]{1,0:T(1,128)S(1)} %bitcast.11), custom_call_target="tpu_custom_call" | custom-call | flops 1000000000 | bytes 3000000 | tf_op jit(solution)/shard_map/slots/pallas_call | solution.py:117
  2.2 0.4 copy-done
  2.6 0.0 copy-start.1
  2.6 1.5 %route.1 = (bf16[8,320,128]{2,1,0:T(8,128)(2,1)S(1)}, bf16[4,320,128]{2,1,0:T(8,128)(2,1)S(1)}, bf16[4,192,128]{2,1,0:T(8,128)(2,1)}, bf16[4,192,128]{2,1,0:T(8,128)(2,1)}) custom-call(s32[1]{0:T(128)} %bitcast.me_ref, bf16[512,512]{1,0:T(8,128)(2,1)S(1)} %get-tuple-element.14.hot_ref, bf16[8,512,128]{2,1,0:T(8,128)(2,1)S(1)} %bitcast.6), custom_call_target="tpu_custom_call" | custom-call | tf_op jit(solution)/shard_map/route/pallas_call | solution.py:147
  4.1 1.5 %collective-permute-start = (bf16[4,320,128]{2,1,0:T(8,128)(2,1)S(1)}, bf16[4,320,128]{2,1,0:T(8,128)(2,1)S(1)}, u32[]{:S(2)}, u32[]{:S(2)}) collective-permute-start(bf16[4,320,128]{2,1,0:T(8,128)(2,1)S(1)} %get-tuple-element.20), channel_id=1, source_target_pairs={{0,64},{8,72},{16,80},{24,88},{32,96},{40,104},{48,112},{56,120},{... | collective-permute-start | bytes 983048 | tf_op jit(solution)/shard_map/ppermute | solution.py:494
  5.6 0.4 collective-permute-start.1
  5.9 1.6 %collective-permute-start.2 = (bf16[4,192,128]{2,1,0:T(8,128)(2,1)}, bf16[4,192,128]{2,1,0:T(8,128)(2,1)S(1)}, u32[]{:S(2)}, u32[]{:S(2)}) collective-permute-start(bf16[4,192,128]{2,1,0:T(8,128)(2,1)} %get-tuple-element.22), channel_id=1, source_target_pairs={{0,72},{8,64},{16,88},{24,80},{32,104},{40,96},{48,120},{56,112},{... | collective-permute-start | bytes 589832 | tf_op jit(solution)/shard_map/ppermute | solution.py:494
  7.6 0.0 copy-done.1
  7.6 0.9 %cut_gains.1 = bf16[8,96,128]{2,1,0:T(8,128)(2,1)} custom-call(s32[1]{0:T(128)} %bitcast.me_ref, f32[8,24,1024]{2,1,0:T(8,128)S(1)} %copy-done.1, bf16[8,320,128]{2,1,0:T(8,128)(2,1)S(1)} %get-tuple-element.15.after_ref.vis_ref), custom_call_target="tpu_custom_call" | custom-call | tf_op jit(solution)/shard_map/cut_gains/pallas_call | solution.py:70
  8.4 0.0 copy-start.2
  8.4 4.6 %all-to-all-start = ((bf16[8,96,128]{2,1,0:T(8,128)(2,1)}), bf16[8,96,128]{2,1,0:T(8,128)(2,1)S(1)}, u32[]{:S(2)}, u32[]{:S(2)}) async-start(bf16[8,96,128]{2,1,0:T(8,128)(2,1)} %cut_gains.1), calls=%async_computation | async-start | bytes 393216 | tf_op jit(solution)/shard_map/all_to_all | solution.py:496
  13.0 0.0 copy-start.4
  13.1 0.0 copy-done.2
  13.1 0.7 %copy-done.4 = s32[512,2]{0,1:T(2,128)S(1)} copy-done((s32[512,2]{0,1:T(2,128)S(1)}, s32[512,2]{0,1:T(2,128)}, u32[]{:S(2)}) %copy-start.4) | copy-done | bytes 4120
  13.7 0.8 %tables.1 = (bf16[320,256]{1,0:T(8,128)(2,1)S(1)}, bf16[320,256]{1,0:T(8,128)(2,1)S(1)}, bf16[256,768]{1,0:T(8,128)(2,1)S(1)}, bf16[128,128]{1,0:T(8,128)(2,1)S(...) custom-call(s32[1]{0:T(128)} %bitcast.me_ref, s32[2,512]{1,0:T(2,128)S(1)} %bitcast.10, s32[2,512]{1,0:T(2,128)S(1)} %bitcast.9, ...), custom_call_target="tpu_custom_call" | custom-call | flops 1000000000 | bytes 4000000 | tf_op jit(solution)/shard_map/tables/pallas_call | solution.py:235
  14.5 5.3 %all-to-all-done.gain_ref = bf16[8,96,128]{2,1,0:T(8,128)(2,1)S(1)} async-done(((bf16[8,96,128]{2,1,0:T(8,128)(2,1)}), bf16[8,96,128]{2,1,0:T(8,128)(2,1)S(1)}, u32[]{:S(2)}, u32[]{:S(2)}) %all-to-all-start) | async-done | bytes 196640 | tf_op jit(solution)/shard_map/all_to_all | solution.py:496
  19.9 0.0 collective-permute-done.1.z_ref
  19.9 0.0 collective-permute-done.2.xz_ref
  19.9 0.0 collective-permute-done.x_ref
  19.9 2.4 %calibrate.1 = bf16[32,80,128]{2,1,0:T(8,128)(2,1)S(1)} custom-call(s32[1]{0:T(128)} %bitcast.me_ref, bf16[8,96,128]{2,1,0:T(8,128)(2,1)S(1)} %all-to-all-done.gain_ref, bf16[320,256]{1,0:T(8,128)(2,1)S(1)} %get-tuple-element.17.left_ref, bf16[320,256]{1,0:T(8,128)(2,1)S(1)} %get-tuple-element.18.right_ref, ...), custom_call_target="tpu_custom_call" | custom-call | tf_op jit(solution)/shard_map/calibrate/pallas_call | solution.py:402
  22.3 31.0 %all_to_all.10.recv_ref = bf16[32,80,128]{2,1,0:T(8,128)(2,1)S(1)} all-to-all(bf16[32,80,128]{2,1,0:T(8,128)(2,1)S(1)} %calibrate.1), channel_id=1, replica_groups=mesh['tm'=32,'chan'=8] {'tm'}, dimensions={0} | all-to-all | bytes 1310720 | tf_op jit(solution)/shard_map/all_to_all | solution.py:499
  53.3 2.9 %finish.1 = (bf16[32,8,16,128]{3,2,1,0:T(8,128)(2,1)}, f32[8,8,128]{2,1,0:T(8,128)}) custom-call(bf16[32,80,128]{2,1,0:T(8,128)(2,1)S(1)} %all_to_all.10.recv_ref, bf16[128,128]{1,0:T(8,128)(2,1)S(1)} %get-tuple-element.23.pick_ref, s32[2,128,128]{2,1,0:T(8,128)S(1)} %get-tuple-element.24.lane_ref, f32[128,128]{1,0:T(8,128)S(1)} %get-tuple-element.25.time_ref), custom_call_target="tpu_custom_call" | custom-call | tf_op jit(solution)/shard_map/finish/pallas_call | solution.py:474
Async XLA Ops:
  0.6 0.7 %copy-start.3 = (s32[512,2]{0,1:T(2,128)S(1)}, s32[512,2]{0,1:T(2,128)}, u32[]{:S(2)}) copy-start(s32[512,2]{0,1:T(2,128)} %param.9) | copy-start | bytes 12292
  0.6 0.7 %copy-start.5 = (s32[512]{0:T(512)S(1)}, s32[512]{0:T(512)}, u32[]{:S(2)}) copy-start(s32[512]{0:T(512)} %param.11) | copy-start | bytes 6148
  1.3 1.2 %copy-start = (bf16[1,8,512,128]{3,2,1,0:T(8,128)(2,1)S(1)}, bf16[1,8,512,128]{3,2,1,0:T(8,128)(2,1)}, u32[]{:S(2)}) copy-start(bf16[1,8,512,128]{3,2,1,0:T(8,128)(2,1)} %param.6) | copy-start | bytes 3145732
  2.6 5.0 %copy-start.1 = (f32[8,24,1024]{2,1,0:T(8,128)S(1)}, f32[8,24,1024]{2,1,0:T(8,128)}, u32[]{:S(2)}) copy-start(f32[8,24,1024]{2,1,0:T(8,128)} %gain_ref.1) | copy-start | bytes 2359300
  4.1 15.8 %collective-permute-start = (bf16[4,320,128]{2,1,0:T(8,128)(2,1)S(1)}, bf16[4,320,128]{2,1,0:T(8,128)(2,1)S(1)}, u32[]{:S(2)}, u32[]{:S(2)}) collective-permute-start(bf16[4,320,128]{2,1,0:T(8,128)(2,1)S(1)} %get-tuple-element.20), channel_id=1, source_target_pairs={{0,64},{8,72},{16,80},{24,88},{32,96},{40,104},{48,112},{56,120},{... | collective-permute-start | bytes 983048 | tf_op jit(solution)/shard_map/ppermute | solution.py:494
  5.6 14.3 %collective-permute-start.1 = (bf16[4,192,128]{2,1,0:T(8,128)(2,1)}, bf16[4,192,128]{2,1,0:T(8,128)(2,1)S(1)}, u32[]{:S(2)}, u32[]{:S(2)}) collective-permute-start(bf16[4,192,128]{2,1,0:T(8,128)(2,1)} %get-tuple-element.21), channel_id=1, source_target_pairs={{0,8},{8,0},{16,24},{24,16},{32,40},{40,32},{48,56},{56,48},{64,72... | collective-permute-start | bytes 589832 | tf_op jit(solution)/shard_map/ppermute | solution.py:494
  5.9 13.9 %collective-permute-start.2 = (bf16[4,192,128]{2,1,0:T(8,128)(2,1)}, bf16[4,192,128]{2,1,0:T(8,128)(2,1)S(1)}, u32[]{:S(2)}, u32[]{:S(2)}) collective-permute-start(bf16[4,192,128]{2,1,0:T(8,128)(2,1)} %get-tuple-element.22), channel_id=1, source_target_pairs={{0,72},{8,64},{16,88},{24,80},{32,104},{40,96},{48,120},{56,112},{... | collective-permute-start | bytes 589832 | tf_op jit(solution)/shard_map/ppermute | solution.py:494
  8.4 4.6 %copy-start.2 = (s32[512,32]{0,1:T(8,128)S(1)}, s32[512,32]{0,1:T(8,128)}, u32[]{:S(2)}) copy-start(s32[512,32]{0,1:T(8,128)} %param.10) | copy-start | bytes 196612
  8.4 11.4 %all-to-all-start = ((bf16[8,96,128]{2,1,0:T(8,128)(2,1)}), bf16[8,96,128]{2,1,0:T(8,128)(2,1)S(1)}, u32[]{:S(2)}, u32[]{:S(2)}) async-start(bf16[8,96,128]{2,1,0:T(8,128)(2,1)} %cut_gains.1), calls=%async_computation | async-start | bytes 393216 | tf_op jit(solution)/shard_map/all_to_all | solution.py:496
  13.0 0.7 %copy-start.4 = (s32[512,2]{0,1:T(2,128)S(1)}, s32[512,2]{0,1:T(2,128)}, u32[]{:S(2)}) copy-start(s32[512,2]{0,1:T(2,128)} %param.8) | copy-start | bytes 12292

commit v6 on v5

--- a/solution.py
+++ b/solution.py
@@ -357,7 +357,7 @@
             block(FIRST[level] + singles + i * 16, other, level)
             return carry
 
-        lax.fori_loop(0, singles // 16, single, 0, unroll=2)
+        lax.fori_loop(0, singles // 16, single, 0, unroll=singles // 16)
         lax.fori_loop(0, 4, paired, 0, unroll=4)
 
     for u in range(3):
@@ -444,13 +444,16 @@
         both = jnp.concatenate([means[first], means[first + 8]], axis=1).astype(BF16)
         rows = dot(pick, both)
         for bit in range(2):
-            half = [
-                jnp.take_along_axis(rows[:, lanes(k)], index[bit], axis=1, mode="promise_in_bounds") for k in range(2)
-            ]
-            avg_ref[first + 8 * bit] = jnp.where(low, half[0], half[1]).astype(BF16).reshape(8, 16, 128)
+            for c in range(8):
+                here = slice(c * 16, (c + 1) * 16)
+                half = [
+                    jnp.take_along_axis(rows[here, lanes(k)], index[bit][here], axis=1, mode="promise_in_bounds")
+                    for k in range(2)
+                ]
+                avg_ref[first + 8 * bit, c] = jnp.where(low[here], half[0], half[1]).astype(BF16)
         return carry
 
-    lax.fori_loop(0, 16, step, 0, unroll=8)
+    lax.fori_loop(0, 16, step, 0, unroll=16)
 
     low8 = low_lanes(8)
     for g in range(4):

time: 56.5 us -> 56.2 us (level)
  no operation moved by 1% of the time
where the time goes in v6:
time: 56.2 us; the launch traced here: 55.8 us
  blocking collectives  31 us (55%)
  Pallas kernels  8.95 us (16%)
  starting transfers between devices  8.09 us (14%)
  waiting for transfers between devices  5.36 us (10%)
  local copies, waits for them, and re-layouts  1.76 us (3%)
  between operations  0.69 us (1%)
    all_to_all x1, blocking collectives, shards(): recv = lax.all_to_all(payload, 'tm', 0, 0, tiled=True)  31 us
    all_to_all x1, waiting for transfers between devices, shards(): lax.all_to_all(cut_gains(me, station_gains, keep), 'chan', 0, 0, tiled=True)  5.35 us
    all_to_all x1, starting transfers between devices, shards(): lax.all_to_all(cut_gains(me, station_gains, keep), 'chan', 0, 0, tiled=True)  4.6 us
    ppermute x3, starting transfers between devices, shards(): lax.ppermute(value, 'tm', [(m, m ^ bits) for m in range(32)])  3.49 us
    pallas_call x1, Pallas kernels, finish(): pl.pallas_call(finish_kernel, in_specs=[vmem] * 4, out_specs=[vmem] * 2,...  2.61 us
    pallas_call x1, Pallas kernels, calibrate(): pl.pallas_call(calibrate_kernel, in_specs=[pl.BlockSpec(memory_space=pltp...  2.33 us
    unnamed x12, local copies, waits for them, and re-layouts  1.76 us
    pallas_call x1, Pallas kernels, route(): pl.pallas_call(route_kernel, in_specs=[pl.BlockSpec(memory_space=pltpu.SM...  1.54 us
  transfers between devices with their start and end apart: 4, of which 1 were waited for; matrix products, arithmetic and copies ran while one was open for 0% of the time, Pallas kernels for 3%

profile of v6, /device:TPU:32, one launch (start us, length us, event | category | flops | bytes accessed | tf_op | source)
XLA Modules:
  0.0 55.8 jit_solution(16672929563313016831)
XLA Ops:
  0.6 0.0 copy-start.3
  0.6 0.0 copy-start.5
  0.7 0.7 %copy-done.3 = s32[512,2]{0,1:T(2,128)S(1)} copy-done((s32[512,2]{0,1:T(2,128)S(1)}, s32[512,2]{0,1:T(2,128)}, u32[]{:S(2)}) %copy-start.3) | copy-done | bytes 4120
  1.3 0.0 copy-done.5
  1.3 0.0 copy-start
  1.3 0.8 %slots.1 = (bf16[512,512]{1,0:T(8,128)(2,1)S(1)}, f32[8,512]{1,0:T(8,128)S(1)}) custom-call(s32[1]{0:T(128)} %bitcast.me_ref, s32[2,512]{1,0:T(2,128)S(1)} %bitcast.8, s32[1,512]{1,0:T(1,128)S(1)} %bitcast.11), custom_call_target="tpu_custom_call" | custom-call | flops 1000000000 | bytes 3000000 | tf_op jit(solution)/shard_map/slots/pallas_call | solution.py:117
  2.2 0.4 copy-done
  2.6 0.0 copy-start.1
  2.6 1.5 %route.1 = (bf16[8,320,128]{2,1,0:T(8,128)(2,1)S(1)}, bf16[4,320,128]{2,1,0:T(8,128)(2,1)S(1)}, bf16[4,192,128]{2,1,0:T(8,128)(2,1)}, bf16[4,192,128]{2,1,0:T(8,128)(2,1)}) custom-call(s32[1]{0:T(128)} %bitcast.me_ref, bf16[512,512]{1,0:T(8,128)(2,1)S(1)} %get-tuple-element.14.hot_ref, bf16[8,512,128]{2,1,0:T(8,128)(2,1)S(1)} %bitcast.6), custom_call_target="tpu_custom_call" | custom-call | tf_op jit(solution)/shard_map/route/pallas_call | solution.py:147
  4.1 1.5 %collective-permute-start = (bf16[4,320,128]{2,1,0:T(8,128)(2,1)S(1)}, bf16[4,320,128]{2,1,0:T(8,128)(2,1)S(1)}, u32[]{:S(2)}, u32[]{:S(2)}) collective-permute-start(bf16[4,320,128]{2,1,0:T(8,128)(2,1)S(1)} %get-tuple-element.20), channel_id=1, source_target_pairs={{0,64},{8,72},{16,80},{24,88},{32,96},{40,104},{48,112},{56,120},{... | collective-permute-start | bytes 983048 | tf_op jit(solution)/shard_map/ppermute | solution.py:497
  5.6 0.4 collective-permute-start.1
  5.9 1.6 %collective-permute-start.2 = (bf16[4,192,128]{2,1,0:T(8,128)(2,1)}, bf16[4,192,128]{2,1,0:T(8,128)(2,1)S(1)}, u32[]{:S(2)}, u32[]{:S(2)}) collective-permute-start(bf16[4,192,128]{2,1,0:T(8,128)(2,1)} %get-tuple-element.22), channel_id=1, source_target_pairs={{0,72},{8,64},{16,88},{24,80},{32,104},{40,96},{48,120},{56,112},{... | collective-permute-start | bytes 589832 | tf_op jit(solution)/shard_map/ppermute | solution.py:497
  7.6 0.0 copy-done.1
  7.6 0.9 %cut_gains.1 = bf16[8,96,128]{2,1,0:T(8,128)(2,1)} custom-call(s32[1]{0:T(128)} %bitcast.me_ref, f32[8,24,1024]{2,1,0:T(8,128)S(1)} %copy-done.1, bf16[8,320,128]{2,1,0:T(8,128)(2,1)S(1)} %get-tuple-element.15.after_ref.vis_ref), custom_call_target="tpu_custom_call" | custom-call | tf_op jit(solution)/shard_map/cut_gains/pallas_call | solution.py:70
  8.4 0.0 copy-start.2
  8.4 4.6 %all-to-all-start = ((bf16[8,96,128]{2,1,0:T(8,128)(2,1)}), bf16[8,96,128]{2,1,0:T(8,128)(2,1)S(1)}, u32[]{:S(2)}, u32[]{:S(2)}) async-start(bf16[8,96,128]{2,1,0:T(8,128)(2,1)} %cut_gains.1), calls=%async_computation | async-start | bytes 393216 | tf_op jit(solution)/shard_map/all_to_all | solution.py:499
  13.0 0.0 copy-start.4
  13.1 0.0 copy-done.2
  13.1 0.7 %copy-done.4 = s32[512,2]{0,1:T(2,128)S(1)} copy-done((s32[512,2]{0,1:T(2,128)S(1)}, s32[512,2]{0,1:T(2,128)}, u32[]{:S(2)}) %copy-start.4) | copy-done | bytes 4120
  13.7 0.8 %tables.1 = (bf16[320,256]{1,0:T(8,128)(2,1)S(1)}, bf16[320,256]{1,0:T(8,128)(2,1)S(1)}, bf16[256,768]{1,0:T(8,128)(2,1)S(1)}, bf16[128,128]{1,0:T(8,128)(2,1)S(...) custom-call(s32[1]{0:T(128)} %bitcast.me_ref, s32[2,512]{1,0:T(2,128)S(1)} %bitcast.10, s32[2,512]{1,0:T(2,128)S(1)} %bitcast.9, ...), custom_call_target="tpu_custom_call" | custom-call | flops 1000000000 | bytes 4000000 | tf_op jit(solution)/shard_map/tables/pallas_call | solution.py:235
  14.5 5.3 %all-to-all-done.gain_ref = bf16[8,96,128]{2,1,0:T(8,128)(2,1)S(1)} async-done(((bf16[8,96,128]{2,1,0:T(8,128)(2,1)}), bf16[8,96,128]{2,1,0:T(8,128)(2,1)S(1)}, u32[]{:S(2)}, u32[]{:S(2)}) %all-to-all-start) | async-done | bytes 196640 | tf_op jit(solution)/shard_map/all_to_all | solution.py:499
  19.9 0.0 collective-permute-done.1.z_ref
  19.9 0.0 collective-permute-done.2.xz_ref
  19.9 0.0 collective-permute-done.x_ref
  19.9 2.3 %calibrate.1 = bf16[32,80,128]{2,1,0:T(8,128)(2,1)S(1)} custom-call(s32[1]{0:T(128)} %bitcast.me_ref, bf16[8,96,128]{2,1,0:T(8,128)(2,1)S(1)} %all-to-all-done.gain_ref, bf16[320,256]{1,0:T(8,128)(2,1)S(1)} %get-tuple-element.17.left_ref, bf16[320,256]{1,0:T(8,128)(2,1)S(1)} %get-tuple-element.18.right_ref, ...), custom_call_target="tpu_custom_call" | custom-call | tf_op jit(solution)/shard_map/calibrate/pallas_call | solution.py:402
  22.2 31.0 %all_to_all.10.recv_ref = bf16[32,80,128]{2,1,0:T(8,128)(2,1)S(1)} all-to-all(bf16[32,80,128]{2,1,0:T(8,128)(2,1)S(1)} %calibrate.1), channel_id=1, replica_groups=mesh['tm'=32,'chan'=8] {'tm'}, dimensions={0} | all-to-all | bytes 1310720 | tf_op jit(solution)/shard_map/all_to_all | solution.py:502
  53.2 2.6 %finish.1 = (bf16[32,8,16,128]{3,2,1,0:T(8,128)(2,1)}, f32[8,8,128]{2,1,0:T(8,128)}) custom-call(bf16[32,80,128]{2,1,0:T(8,128)(2,1)S(1)} %all_to_all.10.recv_ref, bf16[128,128]{1,0:T(8,128)(2,1)S(1)} %get-tuple-element.23.pick_ref, s32[2,128,128]{2,1,0:T(8,128)S(1)} %get-tuple-element.24.lane_ref, f32[128,128]{1,0:T(8,128)S(1)} %get-tuple-element.25.time_ref), custom_call_target="tpu_custom_call" | custom-call | tf_op jit(solution)/shard_map/finish/pallas_call | solution.py:477
Async XLA Ops:
  0.6 0.7 %copy-start.3 = (s32[512,2]{0,1:T(2,128)S(1)}, s32[512,2]{0,1:T(2,128)}, u32[]{:S(2)}) copy-start(s32[512,2]{0,1:T(2,128)} %param.9) | copy-start | bytes 12292
  0.6 0.7 %copy-start.5 = (s32[512]{0:T(512)S(1)}, s32[512]{0:T(512)}, u32[]{:S(2)}) copy-start(s32[512]{0:T(512)} %param.11) | copy-start | bytes 6148
  1.3 1.2 %copy-start = (bf16[1,8,512,128]{3,2,1,0:T(8,128)(2,1)S(1)}, bf16[1,8,512,128]{3,2,1,0:T(8,128)(2,1)}, u32[]{:S(2)}) copy-start(bf16[1,8,512,128]{3,2,1,0:T(8,128)(2,1)} %param.6) | copy-start | bytes 3145732
  2.6 5.0 %copy-start.1 = (f32[8,24,1024]{2,1,0:T(8,128)S(1)}, f32[8,24,1024]{2,1,0:T(8,128)}, u32[]{:S(2)}) copy-start(f32[8,24,1024]{2,1,0:T(8,128)} %gain_ref.1) | copy-start | bytes 2359300
  4.1 15.8 %collective-permute-start = (bf16[4,320,128]{2,1,0:T(8,128)(2,1)S(1)}, bf16[4,320,128]{2,1,0:T(8,128)(2,1)S(1)}, u32[]{:S(2)}, u32[]{:S(2)}) collective-permute-start(bf16[4,320,128]{2,1,0:T(8,128)(2,1)S(1)} %get-tuple-element.20), channel_id=1, source_target_pairs={{0,64},{8,72},{16,80},{24,88},{32,96},{40,104},{48,112},{56,120},{... | collective-permute-start | bytes 983048 | tf_op jit(solution)/shard_map/ppermute | solution.py:497
  5.6 14.3 %collective-permute-start.1 = (bf16[4,192,128]{2,1,0:T(8,128)(2,1)}, bf16[4,192,128]{2,1,0:T(8,128)(2,1)S(1)}, u32[]{:S(2)}, u32[]{:S(2)}) collective-permute-start(bf16[4,192,128]{2,1,0:T(8,128)(2,1)} %get-tuple-element.21), channel_id=1, source_target_pairs={{0,8},{8,0},{16,24},{24,16},{32,40},{40,32},{48,56},{56,48},{64,72... | collective-permute-start | bytes 589832 | tf_op jit(solution)/shard_map/ppermute | solution.py:497
  5.9 13.9 %collective-permute-start.2 = (bf16[4,192,128]{2,1,0:T(8,128)(2,1)}, bf16[4,192,128]{2,1,0:T(8,128)(2,1)S(1)}, u32[]{:S(2)}, u32[]{:S(2)}) collective-permute-start(bf16[4,192,128]{2,1,0:T(8,128)(2,1)} %get-tuple-element.22), channel_id=1, source_target_pairs={{0,72},{8,64},{16,88},{24,80},{32,104},{40,96},{48,120},{56,112},{... | collective-permute-start | bytes 589832 | tf_op jit(solution)/shard_map/ppermute | solution.py:497
  8.4 4.6 %copy-start.2 = (s32[512,32]{0,1:T(8,128)S(1)}, s32[512,32]{0,1:T(8,128)}, u32[]{:S(2)}) copy-start(s32[512,32]{0,1:T(8,128)} %param.10) | copy-start | bytes 196612
  8.4 11.4 %all-to-all-start = ((bf16[8,96,128]{2,1,0:T(8,128)(2,1)}), bf16[8,96,128]{2,1,0:T(8,128)(2,1)S(1)}, u32[]{:S(2)}, u32[]{:S(2)}) async-start(bf16[8,96,128]{2,1,0:T(8,128)(2,1)} %cut_gains.1), calls=%async_computation | async-start | bytes 393216 | tf_op jit(solution)/shard_map/all_to_all | solution.py:499
  13.0 0.7 %copy-start.4 = (s32[512,2]{0,1:T(2,128)S(1)}, s32[512,2]{0,1:T(2,128)}, u32[]{:S(2)}) copy-start(s32[512,2]{0,1:T(2,128)} %param.8) | copy-start | bytes 12292
